TPU v7x, 256 devices: a whole 4x4x8 slice. The times are simulated.
256 devices in a mesh: tm: 4 (over z_hi), space: 64 (over z_lo, x, y, core).
Axes of the slice: x: 4, y: 4, z: 8 (z_hi: 4, z_lo: 2; z = z_hi * 2 + z_lo), core: 2. Of those that a mesh axis runs over, the one named last changes fastest.
Arguments:
- states: float32 [4, 512, 64, 256], P('tm', 'space'), may hold values from -6 to 6
- conductivity: float32 [512, 64, 256], P('space'), may hold values from 0.4 to 1.6
Outputs:
- updated: float32 [4, 512, 64, 256], P('tm', 'space')
All inputs are finite; a program needn't handle non-finite values.
Results may differ from a plain program's by a relative error of at most 0.0001.
Values sent between devices are 32-bit elements; how exact they have to be, the bound alone decides.
No kernel may reach another device: no remote copies, remote signals or barrier semaphores. Data moves between devices by JAX's collectives and lax.ppermute only.
A program may use at most 64 MiB of HBM per device.

v0:
```python
import jax
import jax.numpy as jnp
from jax import lax
from jax.sharding import PartitionSpec as P

FSTEPS = 4


fine_rate = 0.1
coarsen = 4


def with_halo(block, sides, width):
    for axis, dim in sides:
        count = lax.axis_size(axis)
        forward = [(i, i + 1) for i in range(count - 1)]
        backward = [(target, source) for source, target in forward]
        low = lax.ppermute(
            lax.slice_in_dim(block, block.shape[dim] - width, None, axis=dim), axis, forward
        )
        high = lax.ppermute(lax.slice_in_dim(block, 0, width, axis=dim), axis, backward)
        block = jnp.concatenate([low, block, high], axis=dim)
    return block


def passed_along(block, axis, distance):
    devices = range(lax.axis_size(axis))
    route = [(i - distance, i) for i in devices if i - distance in devices]
    return lax.ppermute(block, axis, route)


def plane_div(field, conduct, axis):
    count = field.shape[axis]
    upper = lax.slice_in_dim(field, 1, count, axis=axis)
    lower = lax.slice_in_dim(field, 0, count - 1, axis=axis)
    upper_c = lax.slice_in_dim(conduct, 1, count, axis=axis)
    lower_c = lax.slice_in_dim(conduct, 0, count - 1, axis=axis)
    flux = 0.5 * (upper_c + lower_c) * (upper - lower)
    widths = [(0, 0), (0, 0), (0, 0)]
    widths[axis] = (1, 1)
    padded = jnp.pad(flux, widths)
    return lax.slice_in_dim(padded, 1, count + 1, axis=axis) - lax.slice_in_dim(
        padded, 0, count, axis=axis
    )


def padded_step(padded, conduct, valid, step_rate):
    faces = valid[1:] * valid[:-1]
    flux_z = 0.5 * (conduct[1:] + conduct[:-1]) * (padded[1:] - padded[:-1]) * faces[:, None, None]
    div_z = flux_z[1:] - flux_z[:-1]
    centre = padded[1:-1]
    centre_c = conduct[1:-1]
    div_x = plane_div(centre, centre_c, 1)
    div_y = plane_div(centre, centre_c, 2)
    return centre + step_rate * (div_z + div_x + div_y)


def validity(planes, margin, local_planes):
    first = lax.axis_index("space") * local_planes - margin
    global_plane = first + jnp.arange(planes, dtype=jnp.int32)
    extent = lax.axis_size("space") * local_planes
    return ((global_plane >= 0) & (global_plane < extent)).astype(jnp.float32)


def restrict(field):
    planes, rows, cols = field.shape
    blocks = field.reshape(
        planes // coarsen, coarsen, rows // coarsen, coarsen, cols // coarsen, coarsen
    )
    return jnp.mean(blocks, axis=(1, 3, 5))


def prolong(coarse):
    return jnp.repeat(
        jnp.repeat(jnp.repeat(coarse, coarsen, axis=0), coarsen, axis=1), coarsen, axis=2
    )


def fine_run(field, conduct):
    local_planes = field.shape[0]
    wide_conduct = with_halo(conduct, (("space", 0),), 1)
    valid = validity(local_planes + 2, 1, local_planes)
    for turn in range(FSTEPS):
        padded = with_halo(field, (("space", 0),), 1)
        field = padded_step(padded, wide_conduct, valid, fine_rate)
    return field


def per_device(states, conductivity):
    coarse_rate = fine_rate * FSTEPS / 16.0
    field = states[0]
    fine_end = fine_run(field, conductivity)
    coarse_conduct = restrict(conductivity)
    coarse_planes = coarse_conduct.shape[0]
    padded_conduct = with_halo(coarse_conduct, (("space", 0),), 1)
    coarse_valid = validity(coarse_planes + 2, 1, coarse_planes)

    def propagate(coarse):
        padded = with_halo(coarse, (("space", 0),), 1)
        return padded_step(padded, padded_conduct, coarse_valid, coarse_rate)

    coarse_first = restrict(field)
    coarse_old = propagate(coarse_first)
    jump = restrict(fine_end) - coarse_old
    position = lax.axis_index("tm")
    coarse_new = coarse_old
    carried = coarse_new + jump
    for rounds in range(lax.axis_size("tm") - 1):
        inbound = passed_along(carried, "tm", 1)
        start_state = jnp.where(position == 0, coarse_first, inbound)
        coarse_new = propagate(start_state)
        carried = coarse_new + jump
    result = fine_end + prolong(coarse_new - coarse_old)
    return result[None]


def solution(mesh):
    in_specs = (P("tm", "space", None, None), P("space", None, None))
    out_specs = P("tm", "space", None, None)
    return jax.shard_map(
        per_device, mesh=mesh, in_specs=in_specs, out_specs=out_specs, check_vma=False
    )
```

profile of v0, /device:TPU:95, one launch (start us, length us, event | category | flops | bytes accessed | tf_op | source)
XLA Modules:
  0.0 238.9 jit_solution(4515029153391130947)
XLA Ops:
  0.0 1.5 fusion.83
  1.5 3.7 %collective-permute-start.1 = (f32[1,64,256]{2,1,0:T(8,128)}, f32[1,64,256]{2,1,0:T(8,128)}, u32[]{:S(2)}, u32[]{:S(2)}) collective-permute-start(f32[1,64,256]{2,1,0:T(8,128)} %get-tuple-element.29), channel_id=1, source_target_pairs={{0,1},{1,2},{2,3},{3,4},{4,5},{5,6},{6,7},{7,8},{8,9},{9,10},{10,1... | collective-permute-start | bytes 196616 | tf_op jit(solution)/shard_map/ppermute | solution.py:18
  5.2 19.5 %reshape_squeeze.3 = f32[2,4,16,4,64,4]{5,4,3,2,1,0:T(8,128)} reshape(f32[1,8,64,256]{3,2,1,0:T(8,128)} %param.2) | data formatting | bytes 1048576 | tf_op jit(solution)/shard_map/reshape;squeeze | solution.py:67
  24.7 7.1 %reduce_sum.27 = f32[2,16,64]{2,1,0:T(8,128)S(1)} reduce(f32[2,4,16,4,64,4]{5,4,3,2,1,0:T(8,128)} %reshape_squeeze.3, f32[]{:T(128)} %constant.20.clone.1), dimensions={1,3,5}, to_apply=%region_0.1 | reduce | flops 129024 | bytes 532484 | tf_op jit(solution)/shard_map/reduce_sum | solution.py:70
  31.8 1.9 collective-permute-start.13
  33.7 2.4 %collective-permute-start.12 = (f32[1,16,64]{2,1,0:T(8,128)S(1)}, f32[1,16,64]{2,1,0:T(8,128)S(1)}, u32[]{:S(2)}, u32[]{:S(2)}) collective-permute-start(f32[1,16,64]{2,1,0:T(8,128)S(1)} %get-tuple-element.42), channel_id=1, source_target_pairs={{1,0},{2,1},{3,2},{4,3},{5,4},{6,5},{7,6},{8,7},{9,8},{10,9},{11,1... | collective-permute-start | bytes 12296 | tf_op jit(solution)/shard_map/ppermute | solution.py:21
  36.1 18.6 %reshape.19 = f32[2,4,16,4,64,4]{5,4,3,2,1,0:T(8,128)} reshape(f32[8,64,256]{2,1,0:T(8,128)S(1)} %copy-done) | data formatting | bytes 1048576 | tf_op jit(solution)/shard_map/reshape | solution.py:67
  54.8 7.1 %reduce_sum.28 = f32[2,16,64]{2,1,0:T(8,128)S(1)} reduce(f32[2,4,16,4,64,4]{5,4,3,2,1,0:T(8,128)} %reshape.19, f32[]{:T(128)} %constant.20.clone.1), dimensions={1,3,5}, to_apply=%region_1.2 | reduce | flops 129024 | bytes 532484 | tf_op jit(solution)/shard_map/reduce_sum | solution.py:70
  61.9 2.1 collective-permute-start.10
  63.9 7.7 %collective-permute-start.11 = (f32[1,16,64]{2,1,0:T(8,128)S(1)}, f32[1,16,64]{2,1,0:T(8,128)S(1)}, u32[]{:S(2)}, u32[]{:S(2)}) collective-permute-start(f32[1,16,64]{2,1,0:T(8,128)S(1)} %get-tuple-element.40), channel_id=1, source_target_pairs={{0,1},{1,2},{2,3},{3,4},{4,5},{5,6},{6,7},{7,8},{8,9},{9,10},{10,1... | collective-permute-start | bytes 12296 | tf_op jit(solution)/shard_map/ppermute | solution.py:18
  72.1 0.9 fusion.81
  75.1 2.4 %copy.79 = f32[8,63,256]{1,0,2:T(8,128)} copy(f32[8,63,256]{2,1,0:T(8,128)} %get-tuple-element.23) | data formatting | bytes 1032192
  77.6 1.4 copy.78
  79.0 1.3 copy.81
  80.3 1.4 copy.80
  81.7 3.0 %fusion.23 = (f32[8,63,256]{1,0,2:T(8,128)}, f32[8,63,256]{1,0,2:T(8,128)S(1)}) fusion(f32[8,64,256]{1,0,2:T(8,128)S(1)} %bitcast.11, f32[8,63,256]{1,0,2:T(8,128)} %copy.78, f32[8,63,256]{1,0,2:T(8,128)} %copy.79), kind=kLoop, calls=%fused_computation.35 | loop fusion | flops 516096 | bytes 3096576 | tf_op jit(solution)/shard_map/mul | solution.py:38
  84.7 1.6 fusion.31
  87.9 1.9 collective-permute-start
  90.4 1.9 collective-permute-start.2
  92.3 7.9 %collective-permute-start.3 = (f32[1,64,256]{1,0,2:T(1,128)}, f32[1,64,256]{1,0,2:T(1,128)}, u32[]{:S(2)}, u32[]{:S(2)}) collective-permute-start(f32[1,64,256]{1,0,2:T(1,128)} %bitcast.2), channel_id=1, source_target_pairs={{0,1},{1,2},{2,3},{3,4},{4,5},{5,6},{6,7},{7,8},{8,9},{9,10},{10,1... | collective-permute-start | bytes 196616 | tf_op jit(solution)/shard_map/ppermute | solution.py:18
  101.0 1.8 pad_maximum_fusion.1
  102.8 3.5 %copy.65 = f32[9,64,256]{1,0,2:T(8,128)} copy(f32[9,64,256]{2,1,0:T(8,128)} %get-tuple-element.27) | data formatting | bytes 1179648 | tf_op jit(solution)/shard_map/concatenate | solution.py:22
  106.3 2.5 %copy.64 = f32[9,64,256]{1,0,2:T(8,128)} copy(f32[9,64,256]{2,1,0:T(8,128)S(1)} %get-tuple-element.28) | data formatting | bytes 1179648 | tf_op jit(solution)/shard_map/concatenate | solution.py:22
  108.8 3.1 %fusion.1 = (f32[9,64,256]{1,0,2:T(8,128)S(1)}, f32[9,64,256]{1,0,2:T(8,128)S(1)}) fusion(f32[1,64,256]{1,0,2:T(1,128)S(1)} %collective-permute-done.2, f32[8,64,256]{1,0,2:T(8,128)S(1)} %bitcast.13, f32[1,64,256]{1,0,2:T(1,128)} %collective-permute-done.3, f32[9]{0:T(128)S(1)} %copy-done.11, f32[9,64,256]{1,0,2:T(8,128)} %copy.64, f32[9,64,256]{1,0,2:T(8,128)} %copy.65), kind=kLoop, calls=%fused_computation.2 | loop fusion | flops 1032192 | bytes 3014692 | tf_op jit(solution)/shard_map/mul | solution.py:49
  112.7 2.4 %collective-permute-start.5 = (f32[1,64,256]{1,0,2:T(1,128)S(1)}, f32[1,64,256]{1,0,2:T(1,128)S(1)}, u32[]{:S(2)}, u32[]{:S(2)}) collective-permute-start(f32[1,64,256]{1,0,2:T(1,128)S(1)} %get-tuple-element.21), channel_id=1, source_target_pairs={{0,1},{1,2},{2,3},{3,4},{4,5},{5,6},{6,7},{7,8},{8,9},{9,10},{10,1... | collective-permute-start | bytes 196616 | tf_op jit(solution)/shard_map/ppermute | solution.py:18
  115.1 2.1 collective-permute-start.4
  118.6 7.0 %collective-permute-done.4 = f32[1,64,256]{1,0,2:T(1,128)S(1)} collective-permute-done((f32[1,64,256]{1,0,2:T(1,128)S(1)}, f32[1,64,256]{1,0,2:T(1,128)S(1)}, u32[]{:S(2)}, u32[]{:S(2)}) %collective-permute-start.4) | collective-permute-done | bytes 65568 | tf_op jit(solution)/shard_map/ppermute | solution.py:21
  127.2 1.9 collective-permute-start.7
  129.2 2.4 %collective-permute-start.6 = (f32[1,64,256]{1,0,2:T(1,128)S(1)}, f32[1,64,256]{1,0,2:T(1,128)S(1)}, u32[]{:S(2)}, u32[]{:S(2)}) collective-permute-start(f32[1,64,256]{1,0,2:T(1,128)S(1)} %get-tuple-element.20), channel_id=1, source_target_pairs={{1,0},{2,1},{3,2},{4,3},{5,4},{6,5},{7,6},{8,7},{9,8},{10,9},{11,1... | collective-permute-start | bytes 196616 | tf_op jit(solution)/shard_map/ppermute | solution.py:21
  131.8 7.9 %collective-permute-done.6 = f32[1,64,256]{1,0,2:T(1,128)S(1)} collective-permute-done((f32[1,64,256]{1,0,2:T(1,128)S(1)}, f32[1,64,256]{1,0,2:T(1,128)S(1)}, u32[]{:S(2)}, u32[]{:S(2)}) %collective-permute-start.6) | collective-permute-done | bytes 65568 | tf_op jit(solution)/shard_map/ppermute | solution.py:21
  141.3 1.9 collective-permute-start.9
  143.3 2.4 %collective-permute-start.8 = (f32[1,64,256]{1,0,2:T(1,128)S(1)}, f32[1,64,256]{1,0,2:T(1,128)S(1)}, u32[]{:S(2)}, u32[]{:S(2)}) collective-permute-start(f32[1,64,256]{1,0,2:T(1,128)S(1)} %get-tuple-element.18), channel_id=1, source_target_pairs={{1,0},{2,1},{3,2},{4,3},{5,4},{6,5},{7,6},{8,7},{9,8},{10,9},{11,1... | collective-permute-start | bytes 196616 | tf_op jit(solution)/shard_map/ppermute | solution.py:21
  145.9 7.9 %collective-permute-done.8 = f32[1,64,256]{1,0,2:T(1,128)S(1)} collective-permute-done((f32[1,64,256]{1,0,2:T(1,128)S(1)}, f32[1,64,256]{1,0,2:T(1,128)S(1)}, u32[]{:S(2)}, u32[]{:S(2)}) %collective-permute-start.8) | collective-permute-done | bytes 65568 | tf_op jit(solution)/shard_map/ppermute | solution.py:21
  155.3 18.6 %reshape.20 = f32[2,4,16,4,64,4]{5,4,3,2,1,0:T(8,128)} reshape(f32[8,64,256]{2,1,0:T(8,128)S(1)} %copy.72) | data formatting | bytes 1048576 | tf_op jit(solution)/shard_map/reshape | solution.py:67
  173.9 7.1 %reduce_sum.29 = f32[2,16,64]{2,1,0:T(8,128)S(1)} reduce(f32[2,4,16,4,64,4]{5,4,3,2,1,0:T(8,128)} %reshape.20, f32[]{:T(128)} %constant.20.clone.1), dimensions={1,3,5}, to_apply=%region_2.3 | reduce | flops 129024 | bytes 532484 | tf_op jit(solution)/shard_map/reduce_sum | solution.py:70
  181.1 5.2 %collective-permute-start.14 = (f32[2,16,64]{2,1,0:T(8,128)S(1)}, f32[2,16,64]{2,1,0:T(8,128)S(1)}, u32[]{:S(2)}, u32[]{:S(2)}) collective-permute-start(f32[2,16,64]{2,1,0:T(8,128)S(1)} %get-tuple-element.5), channel_id=1, source_target_pairs={{0,64},{64,128},{128,192},{1,65},{65,129},{129,193},{2,66},{66,130... | collective-permute-start | bytes 24584 | tf_op jit(solution)/shard_map/ppermute | solution.py:29
  187.2 2.6 %collective-permute-start.16 = (f32[1,16,64]{2,1,0:T(8,128)S(1)}, f32[1,16,64]{2,1,0:T(8,128)S(1)}, u32[]{:S(2)}, u32[]{:S(2)}) collective-permute-start(f32[1,16,64]{2,1,0:T(8,128)S(1)} %get-tuple-element.37), channel_id=1, source_target_pairs={{0,1},{1,2},{2,3},{3,4},{4,5},{5,6},{6,7},{7,8},{8,9},{9,10},{10,1... | collective-permute-start | bytes 12296 | tf_op jit(solution)/shard_map/ppermute | solution.py:18
  189.9 1.9 collective-permute-start.15
  191.8 7.2 %collective-permute-done.15 = f32[1,16,64]{2,1,0:T(8,128)S(1)} collective-permute-done((f32[1,16,64]{2,1,0:T(8,128)S(1)}, f32[1,16,64]{2,1,0:T(8,128)S(1)}, u32[]{:S(2)}, u32[]{:S(2)}) %collective-permute-start.15) | collective-permute-done | bytes 4128 | tf_op jit(solution)/shard_map/ppermute | solution.py:21
  199.2 6.0 %collective-permute-start.17 = (f32[2,16,64]{2,1,0:T(8,128)S(1)}, f32[2,16,64]{2,1,0:T(8,128)S(1)}, u32[]{:S(2)}, u32[]{:S(2)}) collective-permute-start(f32[2,16,64]{2,1,0:T(8,128)S(1)} %fusion.51), channel_id=1, source_target_pairs={{0,64},{64,128},{128,192},{1,65},{65,129},{129,193},{2,66},{66,130... | collective-permute-start | bytes 24584 | tf_op jit(solution)/shard_map/ppermute | solution.py:29
  206.2 2.8 %collective-permute-start.19 = (f32[1,16,64]{2,1,0:T(8,128)S(1)}, f32[1,16,64]{2,1,0:T(8,128)S(1)}, u32[]{:S(2)}, u32[]{:S(2)}) collective-permute-start(f32[1,16,64]{2,1,0:T(8,128)S(1)} %get-tuple-element.35), channel_id=1, source_target_pairs={{0,1},{1,2},{2,3},{3,4},{4,5},{5,6},{6,7},{7,8},{8,9},{9,10},{10,1... | collective-permute-start | bytes 12296 | tf_op jit(solution)/shard_map/ppermute | solution.py:18
  209.0 1.9 collective-permute-start.18
  210.9 7.2 %collective-permute-done.18 = f32[1,16,64]{2,1,0:T(8,128)S(1)} collective-permute-done((f32[1,16,64]{2,1,0:T(8,128)S(1)}, f32[1,16,64]{2,1,0:T(8,128)S(1)}, u32[]{:S(2)}, u32[]{:S(2)}) %collective-permute-start.18) | collective-permute-done | bytes 4128 | tf_op jit(solution)/shard_map/ppermute | solution.py:21
  218.3 6.0 %collective-permute-start.20 = (f32[2,16,64]{2,1,0:T(8,128)S(1)}, f32[2,16,64]{2,1,0:T(8,128)S(1)}, u32[]{:S(2)}, u32[]{:S(2)}) collective-permute-start(f32[2,16,64]{2,1,0:T(8,128)S(1)} %fusion.57), channel_id=1, source_target_pairs={{0,64},{64,128},{128,192},{1,65},{65,129},{129,193},{2,66},{66,130... | collective-permute-start | bytes 24584 | tf_op jit(solution)/shard_map/ppermute | solution.py:29
  225.3 2.8 %collective-permute-start.22 = (f32[1,16,64]{2,1,0:T(8,128)S(1)}, f32[1,16,64]{2,1,0:T(8,128)S(1)}, u32[]{:S(2)}, u32[]{:S(2)}) collective-permute-start(f32[1,16,64]{2,1,0:T(8,128)S(1)} %get-tuple-element.33), channel_id=1, source_target_pairs={{0,1},{1,2},{2,3},{3,4},{4,5},{5,6},{6,7},{7,8},{8,9},{9,10},{10,1... | collective-permute-start | bytes 12296 | tf_op jit(solution)/shard_map/ppermute | solution.py:18
  228.1 1.9 collective-permute-start.21
  230.0 7.2 %collective-permute-done.21 = f32[1,16,64]{2,1,0:T(8,128)S(1)} collective-permute-done((f32[1,16,64]{2,1,0:T(8,128)S(1)}, f32[1,16,64]{2,1,0:T(8,128)S(1)}, u32[]{:S(2)}, u32[]{:S(2)}) %collective-permute-start.21) | collective-permute-done | bytes 4128 | tf_op jit(solution)/shard_map/ppermute | solution.py:21
  237.8 1.2 copy.75
  (100 shorter events, 16.6 us)
Async XLA Ops:
  1.5 99.5 %collective-permute-start.1 = (f32[1,64,256]{2,1,0:T(8,128)}, f32[1,64,256]{2,1,0:T(8,128)}, u32[]{:S(2)}, u32[]{:S(2)}) collective-permute-start(f32[1,64,256]{2,1,0:T(8,128)} %get-tuple-element.29), channel_id=1, source_target_pairs={{0,1},{1,2},{2,3},{3,4},{4,5},{5,6},{6,7},{7,8},{8,9},{9,10},{10,1... | collective-permute-start | bytes 196616 | tf_op jit(solution)/shard_map/ppermute | solution.py:18
  24.7 11.5 %copy-start = (f32[8,64,256]{2,1,0:T(8,128)S(1)}, f32[8,64,256]{2,1,0:T(8,128)}, u32[]{:S(2)}) copy-start(f32[8,64,256]{2,1,0:T(8,128)} %param.3) | copy-start | bytes 1572868
  31.8 56.1 %collective-permute-start.13 = (f32[1,16,64]{2,1,0:T(8,128)S(1)}, f32[1,16,64]{2,1,0:T(8,128)S(1)}, u32[]{:S(2)}, u32[]{:S(2)}) collective-permute-start(f32[1,16,64]{2,1,0:T(8,128)S(1)} %get-tuple-element.41), channel_id=1, source_target_pairs={{0,1},{1,2},{2,3},{3,4},{4,5},{5,6},{6,7},{7,8},{8,9},{9,10},{10,1... | collective-permute-start | bytes 12296 | tf_op jit(solution)/shard_map/ppermute | solution.py:18
  33.7 56.1 %collective-permute-start.12 = (f32[1,16,64]{2,1,0:T(8,128)S(1)}, f32[1,16,64]{2,1,0:T(8,128)S(1)}, u32[]{:S(2)}, u32[]{:S(2)}) collective-permute-start(f32[1,16,64]{2,1,0:T(8,128)S(1)} %get-tuple-element.42), channel_id=1, source_target_pairs={{1,0},{2,1},{3,2},{4,3},{5,4},{6,5},{7,6},{8,7},{9,8},{10,9},{11,1... | collective-permute-start | bytes 12296 | tf_op jit(solution)/shard_map/ppermute | solution.py:21
  54.8 16.9 %copy-start.6 = (f32[1,8,64,256]{3,2,1,0:T(8,128)S(1)}, f32[1,8,64,256]{3,2,1,0:T(8,128)}, u32[]{:S(2)}) copy-start(f32[1,8,64,256]{3,2,1,0:T(8,128)} %param.2) | copy-start | bytes 1572868
  61.9 30.4 %collective-permute-start.10 = (f32[1,16,64]{2,1,0:T(8,128)S(1)}, f32[1,16,64]{2,1,0:T(8,128)S(1)}, u32[]{:S(2)}, u32[]{:S(2)}) collective-permute-start(f32[1,16,64]{2,1,0:T(8,128)S(1)} %get-tuple-element.39), channel_id=1, source_target_pairs={{1,0},{2,1},{3,2},{4,3},{5,4},{6,5},{7,6},{8,7},{9,8},{10,9},{11,1... | collective-permute-start | bytes 12296 | tf_op jit(solution)/shard_map/ppermute | solution.py:21
  63.9 36.2 %collective-permute-start.11 = (f32[1,16,64]{2,1,0:T(8,128)S(1)}, f32[1,16,64]{2,1,0:T(8,128)S(1)}, u32[]{:S(2)}, u32[]{:S(2)}) collective-permute-start(f32[1,16,64]{2,1,0:T(8,128)S(1)} %get-tuple-element.40), channel_id=1, source_target_pairs={{0,1},{1,2},{2,3},{3,4},{4,5},{5,6},{6,7},{7,8},{8,9},{9,10},{10,1... | collective-permute-start | bytes 12296 | tf_op jit(solution)/shard_map/ppermute | solution.py:18
  81.7 3.0 %copy-start.3 = (f32[8,64,255]{1,0,2:T(8,128)S(1)}, f32[8,64,255]{1,0,2:T(8,128)}, u32[]{:S(2)}) copy-start(f32[8,64,255]{1,0,2:T(8,128)} %copy.81) | copy-start | bytes 1566724
  81.7 3.0 %copy-start.4 = (f32[8,64,255]{1,0,2:T(8,128)S(1)}, f32[8,64,255]{1,0,2:T(8,128)}, u32[]{:S(2)}) copy-start(f32[8,64,255]{1,0,2:T(8,128)} %copy.80) | copy-start | bytes 1566724
  86.4 14.6 %copy-start.9 = (f32[3]{0:T(128)}, f32[3]{0:T(128)S(1)}, u32[]{:S(2)}) copy-start(f32[3]{0:T(128)S(1)} %slice_multiply_fusion) | copy-start | bytes 40
  87.9 13.1 %collective-permute-start = (f32[1,64,256]{2,1,0:T(8,128)}, f32[1,64,256]{2,1,0:T(8,128)S(1)}, u32[]{:S(2)}, u32[]{:S(2)}) collective-permute-start(f32[1,64,256]{2,1,0:T(8,128)} %get-tuple-element.30), channel_id=1, source_target_pairs={{1,0},{2,1},{3,2},{4,3},{5,4},{6,5},{7,6},{8,7},{9,8},{10,9},{11,1... | collective-permute-start | bytes 196616 | tf_op jit(solution)/shard_map/ppermute | solution.py:21
  89.8 0.6 copy-start.12
  90.4 18.4 %collective-permute-start.2 = (f32[1,64,256]{1,0,2:T(1,128)}, f32[1,64,256]{1,0,2:T(1,128)S(1)}, u32[]{:S(2)}, u32[]{:S(2)}) collective-permute-start(f32[1,64,256]{1,0,2:T(1,128)} %bitcast.1), channel_id=1, source_target_pairs={{1,0},{2,1},{3,2},{4,3},{5,4},{6,5},{7,6},{8,7},{9,8},{10,9},{11,1... | collective-permute-start | bytes 196616 | tf_op jit(solution)/shard_map/ppermute | solution.py:21
  92.3 16.5 %collective-permute-start.3 = (f32[1,64,256]{1,0,2:T(1,128)}, f32[1,64,256]{1,0,2:T(1,128)}, u32[]{:S(2)}, u32[]{:S(2)}) collective-permute-start(f32[1,64,256]{1,0,2:T(1,128)} %bitcast.2), channel_id=1, source_target_pairs={{0,1},{1,2},{2,3},{3,4},{4,5},{5,6},{6,7},{7,8},{8,9},{9,10},{10,1... | collective-permute-start | bytes 196616 | tf_op jit(solution)/shard_map/ppermute | solution.py:18
  102.8 6.0 %copy-start.11 = (f32[9]{0:T(128)S(1)}, f32[9]{0:T(128)}, u32[]{:S(2)}) copy-start(f32[9]{0:T(128)} %slice_multiply_fusion.1) | copy-start | bytes 112
  108.8 3.1 %copy-start.2 = (f32[8,63,256]{1,0,2:T(8,128)S(1)}, f32[8,63,256]{1,0,2:T(8,128)}, u32[]{:S(2)}) copy-start(f32[8,63,256]{1,0,2:T(8,128)} %get-tuple-element.11) | copy-start | bytes 1548292
  108.8 3.1 %copy-start.5 = (f32[8,64,255]{1,0,2:T(8,128)S(1)}, f32[8,64,255]{1,0,2:T(8,128)}, u32[]{:S(2)}) copy-start(f32[8,64,255]{1,0,2:T(8,128)} %get-tuple-element.13) | copy-start | bytes 1566724
  112.7 5.9 %collective-permute-start.5 = (f32[1,64,256]{1,0,2:T(1,128)S(1)}, f32[1,64,256]{1,0,2:T(1,128)S(1)}, u32[]{:S(2)}, u32[]{:S(2)}) collective-permute-start(f32[1,64,256]{1,0,2:T(1,128)S(1)} %get-tuple-element.21), channel_id=1, source_target_pairs={{0,1},{1,2},{2,3},{3,4},{4,5},{5,6},{6,7},{7,8},{8,9},{9,10},{10,1... | collective-permute-start | bytes 196616 | tf_op jit(solution)/shard_map/ppermute | solution.py:18
  115.1 10.5 %collective-permute-start.4 = (f32[1,64,256]{1,0,2:T(1,128)S(1)}, f32[1,64,256]{1,0,2:T(1,128)S(1)}, u32[]{:S(2)}, u32[]{:S(2)}) collective-permute-start(f32[1,64,256]{1,0,2:T(1,128)S(1)} %get-tuple-element.22), channel_id=1, source_target_pairs={{1,0},{2,1},{3,2},{4,3},{5,4},{6,5},{7,6},{8,7},{9,8},{10,9},{11,1... | collective-permute-start | bytes 196616 | tf_op jit(solution)/shard_map/ppermute | solution.py:21
  117.2 1.2 copy-start.1
  127.2 4.5 %collective-permute-start.7 = (f32[1,64,256]{1,0,2:T(1,128)S(1)}, f32[1,64,256]{1,0,2:T(1,128)S(1)}, u32[]{:S(2)}, u32[]{:S(2)}) collective-permute-start(f32[1,64,256]{1,0,2:T(1,128)S(1)} %get-tuple-element.19), channel_id=1, source_target_pairs={{0,1},{1,2},{2,3},{3,4},{4,5},{5,6},{6,7},{7,8},{8,9},{9,10},{10,1... | collective-permute-start | bytes 196616 | tf_op jit(solution)/shard_map/ppermute | solution.py:18
  129.2 10.5 %collective-permute-start.6 = (f32[1,64,256]{1,0,2:T(1,128)S(1)}, f32[1,64,256]{1,0,2:T(1,128)S(1)}, u32[]{:S(2)}, u32[]{:S(2)}) collective-permute-start(f32[1,64,256]{1,0,2:T(1,128)S(1)} %get-tuple-element.20), channel_id=1, source_target_pairs={{1,0},{2,1},{3,2},{4,3},{5,4},{6,5},{7,6},{8,7},{9,8},{10,9},{11,1... | collective-permute-start | bytes 196616 | tf_op jit(solution)/shard_map/ppermute | solution.py:21
  141.3 4.5 %collective-permute-start.9 = (f32[1,64,256]{1,0,2:T(1,128)S(1)}, f32[1,64,256]{1,0,2:T(1,128)S(1)}, u32[]{:S(2)}, u32[]{:S(2)}) collective-permute-start(f32[1,64,256]{1,0,2:T(1,128)S(1)} %get-tuple-element.17), channel_id=1, source_target_pairs={{0,1},{1,2},{2,3},{3,4},{4,5},{5,6},{6,7},{7,8},{8,9},{9,10},{10,1... | collective-permute-start | bytes 196616 | tf_op jit(solution)/shard_map/ppermute | solution.py:18
  143.3 10.5 %collective-permute-start.8 = (f32[1,64,256]{1,0,2:T(1,128)S(1)}, f32[1,64,256]{1,0,2:T(1,128)S(1)}, u32[]{:S(2)}, u32[]{:S(2)}) collective-permute-start(f32[1,64,256]{1,0,2:T(1,128)S(1)} %get-tuple-element.18), channel_id=1, source_target_pairs={{1,0},{2,1},{3,2},{4,3},{5,4},{6,5},{7,6},{8,7},{9,8},{10,9},{11,1... | collective-permute-start | bytes 196616 | tf_op jit(solution)/shard_map/ppermute | solution.py:21
  173.9 7.1 %copy-start.7 = (f32[2,15,64]{2,1,0:T(8,128)S(1)}, f32[2,15,64]{2,1,0:T(8,128)}, u32[]{:S(2)}) copy-start(f32[2,15,64]{2,1,0:T(8,128)} %get-tuple-element.9) | copy-start | bytes 23044
  173.9 7.1 %copy-start.8 = (f32[2,16,63]{2,1,0:T(8,128)S(1)}, f32[2,16,63]{2,1,0:T(8,128)}, u32[]{:S(2)}) copy-start(f32[2,16,63]{2,1,0:T(8,128)} %get-tuple-element.7) | copy-start | bytes 24196
  173.9 25.1 %copy-start.10 = (f32[3]{0:T(128)S(1)}, f32[3]{0:T(128)}, u32[]{:S(2)}) copy-start(f32[3]{0:T(128)} %copy-done.9) | copy-start | bytes 40
  181.1 6.1 %collective-permute-start.14 = (f32[2,16,64]{2,1,0:T(8,128)S(1)}, f32[2,16,64]{2,1,0:T(8,128)S(1)}, u32[]{:S(2)}, u32[]{:S(2)}) collective-permute-start(f32[2,16,64]{2,1,0:T(8,128)S(1)} %get-tuple-element.5), channel_id=1, source_target_pairs={{0,64},{64,128},{128,192},{1,65},{65,129},{129,193},{2,66},{66,130... | collective-permute-start | bytes 24584 | tf_op jit(solution)/shard_map/ppermute | solution.py:29
  187.2 4.6 %collective-permute-start.16 = (f32[1,16,64]{2,1,0:T(8,128)S(1)}, f32[1,16,64]{2,1,0:T(8,128)S(1)}, u32[]{:S(2)}, u32[]{:S(2)}) collective-permute-start(f32[1,16,64]{2,1,0:T(8,128)S(1)} %get-tuple-element.37), channel_id=1, source_target_pairs={{0,1},{1,2},{2,3},{3,4},{4,5},{5,6},{6,7},{7,8},{8,9},{9,10},{10,1... | collective-permute-start | bytes 12296 | tf_op jit(solution)/shard_map/ppermute | solution.py:18
  189.9 9.2 %collective-permute-start.15 = (f32[1,16,64]{2,1,0:T(8,128)S(1)}, f32[1,16,64]{2,1,0:T(8,128)S(1)}, u32[]{:S(2)}, u32[]{:S(2)}) collective-permute-start(f32[1,16,64]{2,1,0:T(8,128)S(1)} %get-tuple-element.38), channel_id=1, source_target_pairs={{1,0},{2,1},{3,2},{4,3},{5,4},{6,5},{7,6},{8,7},{9,8},{10,9},{11,1... | collective-permute-start | bytes 12296 | tf_op jit(solution)/shard_map/ppermute | solution.py:21
  199.2 6.9 %collective-permute-start.17 = (f32[2,16,64]{2,1,0:T(8,128)S(1)}, f32[2,16,64]{2,1,0:T(8,128)S(1)}, u32[]{:S(2)}, u32[]{:S(2)}) collective-permute-start(f32[2,16,64]{2,1,0:T(8,128)S(1)} %fusion.51), channel_id=1, source_target_pairs={{0,64},{64,128},{128,192},{1,65},{65,129},{129,193},{2,66},{66,130... | collective-permute-start | bytes 24584 | tf_op jit(solution)/shard_map/ppermute | solution.py:29
  206.2 4.7 %collective-permute-start.19 = (f32[1,16,64]{2,1,0:T(8,128)S(1)}, f32[1,16,64]{2,1,0:T(8,128)S(1)}, u32[]{:S(2)}, u32[]{:S(2)}) collective-permute-start(f32[1,16,64]{2,1,0:T(8,128)S(1)} %get-tuple-element.35), channel_id=1, source_target_pairs={{0,1},{1,2},{2,3},{3,4},{4,5},{5,6},{6,7},{7,8},{8,9},{9,10},{10,1... | collective-permute-start | bytes 12296 | tf_op jit(solution)/shard_map/ppermute | solution.py:18
  209.0 9.2 %collective-permute-start.18 = (f32[1,16,64]{2,1,0:T(8,128)S(1)}, f32[1,16,64]{2,1,0:T(8,128)S(1)}, u32[]{:S(2)}, u32[]{:S(2)}) collective-permute-start(f32[1,16,64]{2,1,0:T(8,128)S(1)} %get-tuple-element.36), channel_id=1, source_target_pairs={{1,0},{2,1},{3,2},{4,3},{5,4},{6,5},{7,6},{8,7},{9,8},{10,9},{11,1... | collective-permute-start | bytes 12296 | tf_op jit(solution)/shard_map/ppermute | solution.py:21
  218.3 6.9 %collective-permute-start.20 = (f32[2,16,64]{2,1,0:T(8,128)S(1)}, f32[2,16,64]{2,1,0:T(8,128)S(1)}, u32[]{:S(2)}, u32[]{:S(2)}) collective-permute-start(f32[2,16,64]{2,1,0:T(8,128)S(1)} %fusion.57), channel_id=1, source_target_pairs={{0,64},{64,128},{128,192},{1,65},{65,129},{129,193},{2,66},{66,130... | collective-permute-start | bytes 24584 | tf_op jit(solution)/shard_map/ppermute | solution.py:29
  225.3 4.7 %collective-permute-start.22 = (f32[1,16,64]{2,1,0:T(8,128)S(1)}, f32[1,16,64]{2,1,0:T(8,128)S(1)}, u32[]{:S(2)}, u32[]{:S(2)}) collective-permute-start(f32[1,16,64]{2,1,0:T(8,128)S(1)} %get-tuple-element.33), channel_id=1, source_target_pairs={{0,1},{1,2},{2,3},{3,4},{4,5},{5,6},{6,7},{7,8},{8,9},{9,10},{10,1... | collective-permute-start | bytes 12296 | tf_op jit(solution)/shard_map/ppermute | solution.py:18
  228.1 9.2 %collective-permute-start.21 = (f32[1,16,64]{2,1,0:T(8,128)S(1)}, f32[1,16,64]{2,1,0:T(8,128)S(1)}, u32[]{:S(2)}, u32[]{:S(2)}) collective-permute-start(f32[1,16,64]{2,1,0:T(8,128)S(1)} %get-tuple-element.34), channel_id=1, source_target_pairs={{1,0},{2,1},{3,2},{4,3},{5,4},{6,5},{7,6},{8,7},{9,8},{10,9},{11,1... | collective-permute-start | bytes 12296 | tf_op jit(solution)/shard_map/ppermute | solution.py:21
where the time goes:
time: 240 us; the launch traced here: 239 us
  local copies, waits for them, and re-layouts  77.5 us (32%)
  starting transfers between devices  73.8 us (31%)
  waiting for transfers between devices  47 us (20%)
  other arithmetic  40.1 us (17%)
    ppermute x10, waiting for transfers between devices, with_halo(): lax.ppermute(lax.slice_in_dim(block, 0, width, axis=dim), axis, backward)  44.5 us
    reshape x2, local copies, waits for them, and re-layouts, restrict(): field.reshape(planes // coarsen, coarsen, rows // coarsen, coarsen, cols...  37.3 us
    ppermute x10, starting transfers between devices, with_halo(): lax.ppermute(lax.slice_in_dim(block, block.shape[dim] - width, None, axis...  35.6 us
    reduce_sum x3, other arithmetic, restrict(): return jnp.mean(blocks, axis=(1, 3, 5))  21.3 us
    ppermute x10, starting transfers between devices, with_halo(): lax.ppermute(lax.slice_in_dim(block, 0, width, axis=dim), axis, backward)  21 us
    another operation x1, local copies, waits for them, and re-layouts, restrict(): field.reshape(planes // coarsen, coarsen, rows // coarsen, coarsen, cols...  19.5 us
    ppermute x3, starting transfers between devices, passed_along(): return lax.ppermute(block, axis, route)  17.2 us
    unnamed x33, local copies, waits for them, and re-layouts  9.89 us
  transfers between devices with their start and end apart: 23, of which 9 were waited for; matrix products, arithmetic and copies ran while one was open for 33% of the time, Pallas kernels for 0%

commit v1 on v0

v1 whole, which is shorter than its diff:
```python
import jax
import jax.numpy as jnp
from jax import lax
from jax.experimental import pallas as pl
from jax.experimental.pallas import tpu as pltpu
from jax.sharding import PartitionSpec as P

FSTEPS = 4
COARSEN = 4
FINE_RATE = 0.1
COARSE_RATE = FINE_RATE * FSTEPS / 16.0
HALF = 4
F32 = jnp.float32
VMEM_LIMIT = 24 * 1024 * 1024


def roll_up(a, axis):
    return pltpu.roll(a, a.shape[axis] - 1, axis)


def roll_down(a, axis):
    return pltpu.roll(a, 1, axis)


def keep_faces(a, axis):
    at = lax.broadcasted_iota(jnp.int32, a.shape, axis)
    return jnp.where(at < a.shape[axis] - 1, a, 0.0)


def side_coefficients(c, scale):
    kx = keep_faces((c + roll_up(c, 0)) * scale, 0)
    ky = keep_faces((c + roll_up(c, 1)) * scale, 1)
    return kx, ky


def stencil(v, above, below, kz_above, kz_below, kx, ky):
    fx = kx * (roll_up(v, 0) - v)
    fy = ky * (roll_up(v, 1) - v)
    dz = kz_above * (above - v) - kz_below * (v - below)
    dx = fx - roll_down(fx, 0)
    dy = fy - roll_down(fy, 1)
    return v + (dz + dx + dy)


def pooling(rows, cols):
    a = lax.broadcasted_iota(jnp.int32, (rows, cols), 0)
    b = lax.broadcasted_iota(jnp.int32, (rows, cols), 1)
    if rows > cols:
        return jnp.where(a // COARSEN == b, 1.0, 0.0).astype(F32)
    return jnp.where(b // COARSEN == a, 1.0, 0.0).astype(F32)


def dot(a, b):
    return lax.dot_general(
        a, b, (((1,), (0,)), ((), ())), precision=lax.Precision.HIGHEST, preferred_element_type=F32
    )


def pooled(total):
    rows, cols = total.shape
    lanes = dot(total, pooling(cols, cols // COARSEN))
    return dot(pooling(rows // COARSEN, rows), lanes) * (1.0 / COARSEN**3)


def spread(coarse):
    rows, cols = coarse.shape
    tall = dot(pooling(rows * COARSEN, rows), coarse)
    return dot(tall, pooling(cols, cols * COARSEN))


def own_plane(par, i):
    return i + par * (7 - 2 * i)


def fast_plane(par, i):
    return i + par * (3 - 2 * i)


def slow_plane(par, i):
    return (3 - i) + par * (2 * i - 3)


def fill_coefficients(c, kx, ky, kz, lo, hi, face_lo, face_hi, scale):
    @pl.loop(lo, hi)
    def _(p):
        kx[p], ky[p] = side_coefficients(c[p], scale)

    @pl.loop(face_lo, face_hi)
    def _(p):
        kz[p] = (c[p] + c[p + 1]) * scale


def advance(src, dst, shift, kx, ky, kz, lo, hi):
    @pl.loop(lo, hi)
    def _(p):
        dst[p + shift] = stencil(src[p], src[p + 1], src[p - 1], kz[p], kz[p - 1], kx[p], ky[p])


def early_kernel(at, v, c, h, edge, fine, early, v0, c0, w1, w2, w3, kx, ky, kz):
    par = at[0]

    @pl.loop(0, 8)
    def _(i):
        v0[i] = v[own_plane(par, i)]
        c0[i] = c[own_plane(par, i)]

    @pl.loop(0, 4)
    def _(i):
        v0[8 + i] = h[fast_plane(par, i)]
        c0[8 + i] = h[4 + fast_plane(par, i)]

    scale = 0.5 * FINE_RATE
    fill_coefficients(c0, kx, ky, kz, 1, 11, 0, 11, scale)
    advance(v0, w1, 0, kx, ky, kz, 1, 11)
    advance(w1, w2, 0, kx, ky, kz, 2, 10)
    advance(w2, w3, 0, kx, ky, kz, 3, 9)
    advance(w3, fine, -4, kx, ky, kz, 4, 8)
    edge[0] = w1[1]
    edge[1] = w1[2]
    edge[2] = w2[2]
    edge[3] = w2[3]
    edge[4] = w3[3]
    edge[5] = w3[4]
    early[0] = pooled(fine[0] + fine[1] + fine[2] + fine[3])
    for b in range(2):
        early[1 + b] = pooled(v0[4 * b] + v0[4 * b + 1] + v0[4 * b + 2] + v0[4 * b + 3])
        early[3 + b] = pooled(c0[4 * b] + c0[4 * b + 1] + c0[4 * b + 2] + c0[4 * b + 3])


def late_kernel(at, v, c, g, edge, early, theirs, fine, out, v0, c0, w1, w2, w3, kx, ky, kz):
    par = at[0]

    @pl.loop(0, 4)
    def _(i):
        v0[3 - i] = g[slow_plane(par, i)]
        c0[3 - i] = g[4 + slow_plane(par, i)]

    @pl.loop(0, 2)
    def _(i):
        v0[4 + i] = v[own_plane(par, i)]

    @pl.loop(0, 5)
    def _(i):
        c0[4 + i] = c[own_plane(par, i)]

    scale = 0.5 * FINE_RATE
    fill_coefficients(c0, kx, ky, kz, 1, 8, 0, 8, scale)
    kz[3] = jnp.where(at[1] > 0, kz[3], 0.0)
    w1[5] = edge[0]
    w1[6] = edge[1]
    w2[6] = edge[2]
    w2[7] = edge[3]
    w3[7] = edge[4]
    w3[8] = edge[5]
    advance(v0, w1, 0, kx, ky, kz, 1, 5)
    advance(w1, w2, 0, kx, ky, kz, 2, 6)
    advance(w2, w3, 0, kx, ky, kz, 3, 7)
    advance(w3, fine, -4, kx, ky, kz, 4, 8)
    out[0] = pooled(fine[0] + fine[1] + fine[2] + fine[3])
    out[1] = early[0]
    out[2] = theirs[0]
    out[3] = early[1]
    out[4] = early[2]
    out[5] = theirs[2]
    out[6] = early[3]
    out[7] = early[4]
    out[8] = theirs[4]


def final_kernel(at, near, own, other, far, cc, lower, upper, out):
    par, slow_ok, fast_ok, slice_at = at[0], at[1], at[2], at[3]
    scale = 0.5 * COARSE_RATE
    kx, ky, kz = {}, {}, {}
    for p in range(-2, 4):
        kx[p], ky[p] = side_coefficients(cc[p + 3], scale)
    for p in range(-3, 4):
        kz[p] = (cc[p + 3] + cc[p + 4]) * scale
    kz[-1] = jnp.where(slow_ok > 0, kz[-1], 0.0)
    kz[3] = jnp.where(fast_ok > 0, kz[3], 0.0)

    def pick(which, field, p):
        mine, flipped = near[field, p + 3], other[field, 6 - p]
        return jnp.where((par == 0) == (which == 1), mine, flipped)

    def gate(level, a):
        return jnp.where(slice_at >= level, a, 0.0)

    def grow(d, lo, hi):
        return {
            p: stencil(d[p], d[p + 1], d[p - 1], kz[p], kz[p - 1], kx[p], ky[p]) for p in range(lo, hi)
        }

    d = {p: gate(3, far[0, p + 3] - pick(2, 1, p)) for p in range(-3, 5)}
    u = grow(d, -2, 4)
    d = {p: u[p] + gate(2, pick(2, 0, p) - pick(1, 1, p)) for p in range(-2, 4)}
    u = grow(d, -1, 3)
    d = {p: u[p] + gate(1, pick(1, 0, p) - own[1, p + 3]) for p in range(-1, 3)}
    u = grow(d, 0, 2)
    for half, fine in ((0, lower), (1, upper)):
        change = spread(u[half])

        @pl.loop(0, 4)
        def _(i):
            out[own_plane(par, 4 * half + i)] = fine[i] + change


def call(kernel, outs, scratch, flops, count):
    return pl.pallas_call(
        kernel,
        out_shape=[jax.ShapeDtypeStruct(s, F32) for s in outs],
        in_specs=[pl.BlockSpec(memory_space=pltpu.SMEM)]
        + [pl.BlockSpec(memory_space=pltpu.VMEM)] * (count - 1),
        out_specs=[pl.BlockSpec(memory_space=pltpu.VMEM)] * len(outs),
        scratch_shapes=[pltpu.VMEM(s, F32) for s in scratch],
        compiler_params=pltpu.CompilerParams(vmem_limit_bytes=VMEM_LIMIT),
        cost_estimate=pl.CostEstimate(flops=flops, bytes_accessed=flops // 4, transcendentals=0),
    )


def per_device(states, conductivity):
    v, c = states[0], conductivity
    planes, rows, cols = v.shape
    plane = (rows, cols)
    small = (rows // COARSEN, cols // COARSEN)
    k, n = lax.axis_index("space"), lax.axis_index("tm")
    count, slices = lax.axis_size("space"), lax.axis_size("tm")
    par = k % 2
    mate = k + 1 - 2 * par
    inside = lambda i: ((i != 0) & (i != count - 1)).astype(jnp.int32)
    at = jnp.stack([par, inside(k), inside(mate), n]).astype(jnp.int32)

    slow_pairs = [(i, i + 1) for i in range(1, count - 1, 2)]
    slow_pairs += [(b, a) for a, b in slow_pairs]
    fast_pairs = [(i, i ^ 1) for i in range(count)]
    slow = lambda x: lax.ppermute(x, "space", slow_pairs)
    fast = lambda x: lax.ppermute(x, "space", fast_pairs)

    half = lambda a, side: lax.dynamic_slice_in_dim(a, side * HALF, HALF, 0)
    from_slow = slow(jnp.concatenate([half(v, par), half(c, par)]))
    from_fast = fast(jnp.concatenate([half(v, 1 - par), half(c, 1 - par)]))

    edge, upper, early = call(
        early_kernel,
        [(6,) + plane, (4,) + plane, (5,) + small],
        [(12,) + plane] * 8,
        12_000_000,
        4,
    )(at, v, c, from_fast)
    theirs = fast(early)
    lower, coarse = call(
        late_kernel,
        [(4,) + plane, (9,) + small],
        [(10,) + plane] * 8,
        6_000_000,
        7,
    )(at, v, c, from_slow, edge, early, theirs)
    beyond = slow(coarse)
    mate_late = fast(jnp.concatenate([coarse[:1], beyond]))

    def line(mine, mate, at_mine, at_beyond, at_mate):
        return jnp.stack(
            [beyond[at_beyond + 2], beyond[at_beyond + 1], beyond[at_beyond], mine[0], mine[1], mate[0], mate[1]]
            + [mate_late[1 + at_beyond + i] for i in range(3)]
        )

    ends = line((coarse[0], coarse[1]), (theirs[0], mate_late[0]), 0, 0, 0)
    starts = line((early[1], early[2]), (theirs[2], theirs[1]), 0, 3, 0)
    cc = line((early[3], early[4]), (theirs[4], theirs[3]), 0, 6, 0)
    own = jnp.stack([ends, starts])

    pairs = []
    for i in range(count):
        step = 1 + i % 2
        pairs += [(s * count + i, (s + step) * count + i) for s in range(slices - step)]
    near = lax.ppermute(own, ("tm", "space"), pairs)
    far = lax.ppermute(own, "tm", [(0, slices - 1)])
    other = fast(near)
    (result,) = call(final_kernel, [(planes,) + plane], [], 1_000_000, 8)(
        at, near, own, other, far, cc, lower, upper
    )
    return result[None]


def solution(mesh):
    return jax.shard_map(
        per_device,
        mesh=mesh,
        in_specs=(P("tm", "space", None, None), P("space", None, None)),
        out_specs=P("tm", "space", None, None),
        check_vma=False,
    )
```

time: 240 us -> 53.8 us (0.22)
  the two profiles are of different devices: /device:TPU:95 before, /device:TPU:7 now
where the time goes in v1:
time: 53.8 us; the launch traced here: 53.6 us
  starting transfers between devices  20.8 us (39%)
  waiting for transfers between devices  15.6 us (29%)
  Pallas kernels  15.6 us (29%)
  local copies, waits for them, and re-layouts  1.27 us (2%)
    ppermute x1, waiting for transfers between devices, per_device(): far = lax.ppermute(own, 'tm', [(0, slices - 1)])  9.16 us
    ppermute x1, starting transfers between devices, per_device(): near = lax.ppermute(own, ('tm', 'space'), pairs)  8.82 us
    pallas_call x1, Pallas kernels, per_device(): call(early_kernel, [(6,) + plane, (4,) + plane, (5,) + small], [(12,) + p...  7.73 us
    ppermute x4, starting transfers between devices, per_device(): fast = lambda x: lax.ppermute(x, 'space', fast_pairs)  5.51 us
    ppermute x2, starting transfers between devices, per_device(): slow = lambda x: lax.ppermute(x, 'space', slow_pairs)  5.21 us
    pallas_call x1, Pallas kernels, per_device(): call(late_kernel, [(4,) + plane, (9,) + small], [(10,) + plane] * 8, 6000...  4.48 us
    ppermute x2, waiting for transfers between devices, per_device(): slow = lambda x: lax.ppermute(x, 'space', slow_pairs)  3.74 us
    pallas_call x1, Pallas kernels, per_device(): call(final_kernel, [(planes,) + plane], [], 1000000, 8)  3.37 us
  transfers between devices with their start and end apart: 8, of which 5 were waited for; matrix products, arithmetic and copies ran while one was open for 0% of the time, Pallas kernels for 14%

profile of v1, /device:TPU:7, one launch (start us, length us, event | category | flops | bytes accessed | tf_op | source)
XLA Modules:
  0.0 53.6 jit_solution(8756950435937229326)
XLA Ops:
  0.0 0.0 copy-start.1
  0.0 1.1 %dynamic-slice_bitcast_fusion = (f32[4,64,256]{2,1,0:T(8,128)S(1)}, f32[4,64,256]{2,1,0:T(8,128)S(1)}) fusion(f32[1,8,64,256]{3,2,1,0:T(8,128)} %param.2, s32[]{:T(128)S(6)} %select_n.17, s32[]{:T(128)S(6)} %select_n.16), kind=kLoop, calls=%fused_computation.2 | loop fusion | bytes 1048584 | tf_op jit(solution)/shard_map/dynamic_slice | solution.py:238
  1.1 0.1 copy-done.1
  1.3 0.8 %collective-permute-start.1 = (f32[8,64,256]{2,1,0:T(8,128)S(1)}, f32[8,64,256]{2,1,0:T(8,128)S(1)}, u32[]{:S(2)}, u32[]{:S(2)}) collective-permute-start(f32[8,64,256]{2,1,0:T(8,128)S(1)} %pad_maximum_fusion.1), channel_id=1, source_target_pairs={{0,1},{1,0},{2,3},{3,2},{4,5},{5,4},{6,7},{7,6},{8,9},{9,8},{10,11... | collective-permute-start | bytes 1572872 | tf_op jit(solution)/shard_map/ppermute | solution.py:236
  2.0 0.0 copy-start
  2.1 3.3 %collective-permute-start = (f32[8,64,256]{2,1,0:T(8,128)S(1)}, f32[8,64,256]{2,1,0:T(8,128)S(1)}, u32[]{:S(2)}, u32[]{:S(2)}) collective-permute-start(f32[8,64,256]{2,1,0:T(8,128)S(1)} %pad_maximum_fusion), channel_id=1, source_target_pairs={{1,2},{3,4},{5,6},{7,8},{9,10},{11,12},{13,14},{15,16},{17,18},{19... | collective-permute-start | bytes 1572872 | tf_op jit(solution)/shard_map/ppermute | solution.py:235
  5.4 0.1 pad_add_fusion.at
  5.4 0.0 collective-permute-done.1.h
  5.4 0.0 copy-done
  5.4 7.7 %shard_map.28 = (f32[6,64,256]{2,1,0:T(8,128)S(1)}, f32[4,64,256]{2,1,0:T(8,128)S(1)}, f32[5,16,64]{2,1,0:T(8,128)S(1)}) custom-call(s32[4]{0:T(128)S(1)} %pad_add_fusion.at, f32[8,64,256]{2,1,0:T(8,128)S(1)} %bitcast.12, f32[8,64,256]{2,1,0:T(8,128)S(1)} %copy-done.1, f32[8,64,256]{2,1,0:T(8,128)S(1)} %collective-permute-done.1.h), custom_call_target="tpu_custom_call" | custom-call | flops 12000000 | bytes 3000000 | tf_op jit(solution)/shard_map/pallas_call | solution.py:242
  13.2 2.2 %collective-permute-start.2 = (f32[5,16,64]{2,1,0:T(8,128)S(1)}, f32[5,16,64]{2,1,0:T(8,128)S(1)}, u32[]{:S(2)}, u32[]{:S(2)}) collective-permute-start(f32[5,16,64]{2,1,0:T(8,128)S(1)} %get-tuple-element.11.early), channel_id=1, source_target_pairs={{0,1},{1,0},{2,3},{3,2},{4,5},{5,4},{6,7},{7,6},{8,9},{9,8},{10,11... | collective-permute-start | bytes 61448 | tf_op jit(solution)/shard_map/ppermute | solution.py:236
  15.4 0.0 collective-permute-done.g
  15.4 0.9 %collective-permute-done.2.theirs = f32[5,16,64]{2,1,0:T(8,128)S(1)} collective-permute-done((f32[5,16,64]{2,1,0:T(8,128)S(1)}, f32[5,16,64]{2,1,0:T(8,128)S(1)}, u32[]{:S(2)}, u32[]{:S(2)}) %collective-permute-start.2) | collective-permute-done | bytes 20512 | tf_op jit(solution)/shard_map/ppermute | solution.py:236
  16.2 4.5 %shard_map.29 = (f32[4,64,256]{2,1,0:T(8,128)S(1)}, f32[9,16,64]{2,1,0:T(8,128)S(1)}) custom-call(s32[4]{0:T(128)S(1)} %pad_add_fusion.at, f32[8,64,256]{2,1,0:T(8,128)S(1)} %bitcast.13, f32[8,64,256]{2,1,0:T(8,128)S(1)} %copy-done.1, f32[8,64,256]{2,1,0:T(8,128)S(1)} %collective-permute-done.g, f32[6,64,256]{2,1,0:T(8,128)S(1)} %get-tuple-element.10.edge, ...), custom_call_target="tpu_custom_call" | custom-call | flops 6000000 | bytes 1500000 | tf_op jit(solution)/shard_map/pallas_call | solution.py:250
  20.7 2.0 %collective-permute-start.3 = (f32[9,16,64]{2,1,0:T(8,128)S(1)}, f32[9,16,64]{2,1,0:T(8,128)S(1)}, u32[]{:S(2)}, u32[]{:S(2)}) collective-permute-start(f32[9,16,64]{2,1,0:T(8,128)S(1)} %get-tuple-element.12), channel_id=1, source_target_pairs={{1,2},{3,4},{5,6},{7,8},{9,10},{11,12},{13,14},{15,16},{17,18},{19... | collective-permute-start | bytes 110600 | tf_op jit(solution)/shard_map/ppermute | solution.py:235
  22.7 3.7 %collective-permute-done.3 = f32[9,16,64]{2,1,0:T(8,128)S(1)} collective-permute-done((f32[9,16,64]{2,1,0:T(8,128)S(1)}, f32[9,16,64]{2,1,0:T(8,128)S(1)}, u32[]{:S(2)}, u32[]{:S(2)}) %collective-permute-start.3) | collective-permute-done | bytes 36896 | tf_op jit(solution)/shard_map/ppermute | solution.py:235
  26.5 2.5 %collective-permute-start.4 = (f32[10,16,64]{2,1,0:T(8,128)S(1)}, f32[10,16,64]{2,1,0:T(8,128)S(1)}, u32[]{:S(2)}, u32[]{:S(2)}) collective-permute-start(f32[10,16,64]{2,1,0:T(8,128)S(1)} %pad_maximum_fusion.3), channel_id=1, source_target_pairs={{0,1},{1,0},{2,3},{3,2},{4,5},{5,4},{6,7},{7,6},{8,9},{9,8},{10,11... | collective-permute-start | bytes 122888 | tf_op jit(solution)/shard_map/ppermute | solution.py:236
  29.1 0.9 %collective-permute-done.4 = f32[10,16,64]{2,1,0:T(8,128)S(1)} collective-permute-done((f32[10,16,64]{2,1,0:T(8,128)S(1)}, f32[10,16,64]{2,1,0:T(8,128)S(1)}, u32[]{:S(2)}, u32[]{:S(2)}) %collective-permute-start.4) | collective-permute-done | bytes 40992 | tf_op jit(solution)/shard_map/ppermute | solution.py:236
  30.0 8.8 %collective-permute-start.5 = (f32[2,10,16,64]{3,2,1,0:T(8,128)S(1)}, f32[2,10,16,64]{3,2,1,0:T(8,128)S(1)}, u32[]{:S(2)}, u32[]{:S(2)}) collective-permute-start(f32[2,10,16,64]{3,2,1,0:T(8,128)S(1)} %pad_maximum_fusion.2.own), channel_id=1, source_target_pairs={{0,64},{64,128},{128,192},{1,129},{65,193},{2,66},{66,130},{130,19... | collective-permute-start | bytes 245768 | tf_op jit(solution)/shard_map/ppermute | solution.py:275
  38.8 1.3 %collective-permute-start.7 = (f32[2,10,16,64]{3,2,1,0:T(8,128)S(1)}, f32[2,10,16,64]{3,2,1,0:T(8,128)S(1)}, u32[]{:S(2)}, u32[]{:S(2)}) collective-permute-start(f32[2,10,16,64]{3,2,1,0:T(8,128)S(1)} %pad_maximum_fusion.2.own), channel_id=1, source_target_pairs={{0,192},{1,193},{2,194},{3,195},{4,196},{5,197},{6,198},{7,199},{8... | collective-permute-start | bytes 245768 | tf_op jit(solution)/shard_map/ppermute | solution.py:276
  40.1 1.0 %collective-permute-done.5.near = f32[2,10,16,64]{3,2,1,0:T(8,128)S(1)} collective-permute-done((f32[2,10,16,64]{3,2,1,0:T(8,128)S(1)}, f32[2,10,16,64]{3,2,1,0:T(8,128)S(1)}, u32[]{:S(2)}, u32[]{:S(2)}) %collective-permute-start.5) | collective-permute-done | bytes 81952 | tf_op jit(solution)/shard_map/ppermute | solution.py:275
  41.1 0.0 collective-permute-start.6
  41.1 9.2 %collective-permute-done.7.far = f32[2,10,16,64]{3,2,1,0:T(8,128)S(1)} collective-permute-done((f32[2,10,16,64]{3,2,1,0:T(8,128)S(1)}, f32[2,10,16,64]{3,2,1,0:T(8,128)S(1)}, u32[]{:S(2)}, u32[]{:S(2)}) %collective-permute-start.7) | collective-permute-done | bytes 81952 | tf_op jit(solution)/shard_map/ppermute | solution.py:276
  50.3 0.0 collective-permute-done.6.other
  50.3 3.4 %shard_map.30 = f32[8,64,256]{2,1,0:T(8,128)} custom-call(s32[4]{0:T(128)S(1)} %pad_add_fusion.at, f32[2,10,16,64]{3,2,1,0:T(8,128)S(1)} %collective-permute-done.5.near, f32[2,10,16,64]{3,2,1,0:T(8,128)S(1)} %pad_maximum_fusion.2.own, f32[2,10,16,64]{3,2,1,0:T(8,128)S(1)} %collective-permute-done.6.other, f32[2,10,16,64]{3,2,1,0:T(8,128)S(1)} %collective-permute-done.7.far, ...), custom_call_target="tpu_custom_call" | custom-call | flops 1000000 | bytes 250000 | tf_op jit(solution)/shard_map/pallas_call | solution.py:278
  (15 shorter events, 0.2 us)
Async XLA Ops:
  0.0 1.2 %copy-start.1 = (f32[8,64,256]{2,1,0:T(8,128)S(1)}, f32[8,64,256]{2,1,0:T(8,128)}, u32[]{:S(2)}) copy-start(f32[8,64,256]{2,1,0:T(8,128)} %c.3) | copy-start | bytes 1572868
  1.3 4.2 %collective-permute-start.1 = (f32[8,64,256]{2,1,0:T(8,128)S(1)}, f32[8,64,256]{2,1,0:T(8,128)S(1)}, u32[]{:S(2)}, u32[]{:S(2)}) collective-permute-start(f32[8,64,256]{2,1,0:T(8,128)S(1)} %pad_maximum_fusion.1), channel_id=1, source_target_pairs={{0,1},{1,0},{2,3},{3,2},{4,5},{5,4},{6,7},{7,6},{8,9},{9,8},{10,11... | collective-permute-start | bytes 1572872 | tf_op jit(solution)/shard_map/ppermute | solution.py:236
  2.0 3.4 %copy-start = (f32[1,8,64,256]{3,2,1,0:T(8,128)S(1)}, f32[1,8,64,256]{3,2,1,0:T(8,128)}, u32[]{:S(2)}) copy-start(f32[1,8,64,256]{3,2,1,0:T(8,128)} %param.2) | copy-start | bytes 1572868
  2.1 13.3 %collective-permute-start = (f32[8,64,256]{2,1,0:T(8,128)S(1)}, f32[8,64,256]{2,1,0:T(8,128)S(1)}, u32[]{:S(2)}, u32[]{:S(2)}) collective-permute-start(f32[8,64,256]{2,1,0:T(8,128)S(1)} %pad_maximum_fusion), channel_id=1, source_target_pairs={{1,2},{3,4},{5,6},{7,8},{9,10},{11,12},{13,14},{15,16},{17,18},{19... | collective-permute-start | bytes 1572872 | tf_op jit(solution)/shard_map/ppermute | solution.py:235
  13.2 3.1 %collective-permute-start.2 = (f32[5,16,64]{2,1,0:T(8,128)S(1)}, f32[5,16,64]{2,1,0:T(8,128)S(1)}, u32[]{:S(2)}, u32[]{:S(2)}) collective-permute-start(f32[5,16,64]{2,1,0:T(8,128)S(1)} %get-tuple-element.11.early), channel_id=1, source_target_pairs={{0,1},{1,0},{2,3},{3,2},{4,5},{5,4},{6,7},{7,6},{8,9},{9,8},{10,11... | collective-permute-start | bytes 61448 | tf_op jit(solution)/shard_map/ppermute | solution.py:236
  20.7 5.7 %collective-permute-start.3 = (f32[9,16,64]{2,1,0:T(8,128)S(1)}, f32[9,16,64]{2,1,0:T(8,128)S(1)}, u32[]{:S(2)}, u32[]{:S(2)}) collective-permute-start(f32[9,16,64]{2,1,0:T(8,128)S(1)} %get-tuple-element.12), channel_id=1, source_target_pairs={{1,2},{3,4},{5,6},{7,8},{9,10},{11,12},{13,14},{15,16},{17,18},{19... | collective-permute-start | bytes 110600 | tf_op jit(solution)/shard_map/ppermute | solution.py:235
  26.5 3.5 %collective-permute-start.4 = (f32[10,16,64]{2,1,0:T(8,128)S(1)}, f32[10,16,64]{2,1,0:T(8,128)S(1)}, u32[]{:S(2)}, u32[]{:S(2)}) collective-permute-start(f32[10,16,64]{2,1,0:T(8,128)S(1)} %pad_maximum_fusion.3), channel_id=1, source_target_pairs={{0,1},{1,0},{2,3},{3,2},{4,5},{5,4},{6,7},{7,6},{8,9},{9,8},{10,11... | collective-permute-start | bytes 122888 | tf_op jit(solution)/shard_map/ppermute | solution.py:236
  30.0 11.1 %collective-permute-start.5 = (f32[2,10,16,64]{3,2,1,0:T(8,128)S(1)}, f32[2,10,16,64]{3,2,1,0:T(8,128)S(1)}, u32[]{:S(2)}, u32[]{:S(2)}) collective-permute-start(f32[2,10,16,64]{3,2,1,0:T(8,128)S(1)} %pad_maximum_fusion.2.own), channel_id=1, source_target_pairs={{0,64},{64,128},{128,192},{1,129},{65,193},{2,66},{66,130},{130,19... | collective-permute-start | bytes 245768 | tf_op jit(solution)/shard_map/ppermute | solution.py:275
  38.8 11.5 %collective-permute-start.7 = (f32[2,10,16,64]{3,2,1,0:T(8,128)S(1)}, f32[2,10,16,64]{3,2,1,0:T(8,128)S(1)}, u32[]{:S(2)}, u32[]{:S(2)}) collective-permute-start(f32[2,10,16,64]{3,2,1,0:T(8,128)S(1)} %pad_maximum_fusion.2.own), channel_id=1, source_target_pairs={{0,192},{1,193},{2,194},{3,195},{4,196},{5,197},{6,198},{7,199},{8... | collective-permute-start | bytes 245768 | tf_op jit(solution)/shard_map/ppermute | solution.py:276
  41.1 9.2 %collective-permute-start.6 = (f32[2,10,16,64]{3,2,1,0:T(8,128)S(1)}, f32[2,10,16,64]{3,2,1,0:T(8,128)S(1)}, u32[]{:S(2)}, u32[]{:S(2)}) collective-permute-start(f32[2,10,16,64]{3,2,1,0:T(8,128)S(1)} %collective-permute-done.5.near), channel_id=1, source_target_pairs={{0,1},{1,0},{2,3},{3,2},{4,5},{5,4},{6,7},{7,6},{8,9},{9,8},{10,11... | collective-permute-start | bytes 245768 | tf_op jit(solution)/shard_map/ppermute | solution.py:236

commit v2 on v1

v2 whole, which is shorter than its diff:
```python
import jax
import jax.numpy as jnp
from jax import lax
from jax.experimental import pallas as pl
from jax.experimental.pallas import tpu as pltpu
from jax.sharding import PartitionSpec as P


FSTEPS = 4
COARSEN = 4
FINE_RATE = 0.1
COARSE_RATE = FINE_RATE * FSTEPS / 16.0
HALF = 4
F32 = jnp.float32
BF16 = jnp.bfloat16
VMEM_LIMIT = 24 * 1024 * 1024
PACK_LIMIT = VMEM_LIMIT
LANES = 128
ROWS = 64
TOP = 8
PADDED = 80
UNROLL = True
CHUNK = 8


def own_plane(par, i):
    return i + par * (7 - 2 * i)


def fast_plane(par, i):
    return i + par * (3 - 2 * i)


def slow_plane(par, i):
    return (3 - i) + par * (2 * i - 3)


def rows_of(ref, p, h, shift=0):
    return ref[p, h, TOP + shift : TOP + ROWS + shift, :]


def put(ref, p, plane):
    for h in range(2):
        ref[p, h, TOP : TOP + ROWS, :] = plane[:, h * LANES : (h + 1) * LANES]


def blank_margins(ref, planes):
    for p in range(planes):
        for h in range(2):
            ref[p, h, 0:TOP, :] = jnp.zeros((TOP, LANES), F32)
            ref[p, h, TOP + ROWS : PADDED, :] = jnp.zeros((TOP, LANES), F32)


def mirror_margins(ref, p):
    for h in range(2):
        ref[p, h, TOP - 1 : TOP, :] = -ref[p, h, TOP : TOP + 1, :]
        ref[p, h, TOP + ROWS : TOP + ROWS + 1, :] = -ref[p, h, TOP + ROWS - 1 : TOP + ROWS, :]


def lane_turns(a0, a1):
    at = lax.broadcasted_iota(jnp.int32, a0.shape, 1)
    up0, up1 = pltpu.roll(a0, LANES - 1, 1), pltpu.roll(a1, LANES - 1, 1)
    down0, down1 = pltpu.roll(a0, 1, 1), pltpu.roll(a1, 1, 1)
    return (jnp.where(at == LANES - 1, up1, up0), up1), (down0, jnp.where(at == 0, down0, down1)), at


def fill_faces(c, kz, lo, hi, scale, unroll):
    @pl.loop(lo, hi, unroll=unroll)
    def _(p):
        for h in range(2):
            kz[p, h] = (rows_of(c, p, h) + rows_of(c, p + 1, h)) * scale


def fill_coefficients(c, kz, k, lo, hi, scale, unroll):
    @pl.loop(lo, hi, unroll=unroll)
    def _(p):
        a0, a1 = rows_of(c, p, 0), rows_of(c, p, 1)
        (up0, up1), (down0, down1), at = lane_turns(a0, a1)
        up1 = jnp.where(at == LANES - 1, -a1, up1)
        down0 = jnp.where(at == 0, -a0, down0)
        for h, a, up, down in ((0, a0, up0, down0), (1, a1, up1, down1)):
            kxu = (a + rows_of(c, p, h, 1)) * scale
            kxd = (a + rows_of(c, p, h, -1)) * scale
            kyu = (a + up) * scale
            kyd = (a + down) * scale
            k[p, 0, h] = 1.0 - ((kxu + kxd) + (kyu + kyd) + (kz[p, h] + kz[p - 1, h]))
            k[p, 1, h] = kxu
            k[p, 2, h] = kxd
            k[p, 3, h] = kyu
            k[p, 4, h] = kyd


def advance(src, store, kz, k, lo, hi, unroll, shift=0):
    at = lax.broadcasted_iota(jnp.int32, (CHUNK, LANES), 1)

    def some(p):
        q = p - shift
        made = []
        for r in range(0, ROWS, CHUNK):
            cut = lambda ref, i, h, s=0: ref[i, h, TOP + r + s : TOP + r + s + CHUNK, :]
            w = lambda i, h: k[q, i, h, r : r + CHUNK, :]
            v = [cut(src, p, h) for h in range(2)]
            up = [pltpu.roll(v[h], LANES - 1, 1) for h in range(2)]
            down = [pltpu.roll(v[h], 1, 1) for h in range(2)]
            up = [jnp.where(at == LANES - 1, up[1], up[0]), up[1]]
            down = [down[0], jnp.where(at == 0, down[0], down[1])]
            for h in range(2):
                a = w(0, h) * v[h]
                b = kz[q, h, r : r + CHUNK] * cut(src, p + 1, h) + kz[q - 1, h, r : r + CHUNK] * cut(src, p - 1, h)
                d = w(1, h) * cut(src, p, h, 1) + w(2, h) * cut(src, p, h, -1)
                e = w(3, h) * up[h] + w(4, h) * down[h]
                made.append((r, h, (a + b) + (d + e)))
        return made

    @pl.loop(lo, hi, unroll=unroll)
    def _(p):
        for r, h, a in some(p):
            store(p, h, r, a)


def into(ref):
    def store(p, h, r, a):
        ref[p, h, TOP + r : TOP + r + CHUNK, :] = a

    return store


def into_fine(ref, shift):
    def store(p, h, r, a):
        ref[p - shift, h, r : r + CHUNK, :] = a

    return store


def block_sums(ref, first, top):
    parts = []
    for side in range(2):
        for h in range(2):
            total = None
            for p in range(first, first + COARSEN):
                for r in range(COARSEN):
                    term = ref[p, h, pl.ds(top + 32 * side + r, 8, stride=COARSEN), :]
                    total = term if total is None else total + term
            parts.append(total)
    return jnp.concatenate(parts, axis=1)


def mxu(a, b):
    return lax.dot_general(a, b, (((1,), (0,)), ((), ())), preferred_element_type=F32)


def split_dot(a, b):
    high = a.astype(BF16)
    low = (a - high.astype(F32)).astype(BF16)
    return mxu(high, b) + mxu(low, b)


def pooled(sums, pool):
    return split_dot(sums, pool) * (1.0 / COARSEN**3)


def pack_kernel(at, v, c, near_slow, near_fast, sems):
    par = at[0]
    copies = []
    for s, (ref, side) in enumerate(((near_slow, par), (near_fast, 1 - par))):
        for f, src in enumerate((v, c)):
            copies.append(
                pltpu.make_async_copy(
                    src.at[pl.ds(side * HALF, HALF)], ref.at[pl.ds(f * HALF, HALF)], sems.at[2 * s + f]
                )
            )
    for copy in copies:
        copy.start()
    for copy in copies:
        copy.wait()


def put_own(par, near_slow, near_fast, field, coefficient):
    @pl.loop(0, 4)
    def _(i):
        for base, ref in ((0, near_slow), (4, near_fast)):
            put(field, base + i, ref[fast_plane(par, i)])
            put(coefficient, base + i, ref[HALF + fast_plane(par, i)])


def coarse_kernel(at, near_slow, near_fast, pool, out, v0, c0):
    put_own(at[0], near_slow, near_fast, v0, c0)
    sums = [block_sums(ref, 4 * b, TOP) for ref in (v0, c0) for b in range(2)]
    res = pooled(jnp.concatenate(sums, axis=0), pool[...])
    for i in range(4):
        out[i] = res[8 * i : 8 * i + 8]


def early_kernel(at, near_slow, near_fast, h, pool, own, theirs, a, b, kz, k, fine, end, starts, c0):
    par = at[0]
    blank_margins(a, 12)
    blank_margins(b, 12)
    put_own(par, near_slow, near_fast, a, c0)

    @pl.loop(0, 4)
    def _(i):
        put(a, 8 + i, h[fast_plane(par, i)])
        put(c0, 8 + i, h[HALF + fast_plane(par, i)])

    for i in range(12):
        mirror_margins(c0, i)
    scale = 0.5 * FINE_RATE
    fill_faces(c0, kz, 0, 11, scale, UNROLL)
    fill_coefficients(c0, kz, k, 1, 11, scale, UNROLL)
    advance(a, into(b), kz, k, 1, 11, UNROLL)
    advance(b, into(a), kz, k, 2, 10, UNROLL)
    advance(a, into(b), kz, k, 3, 9, UNROLL)
    advance(b, into_fine(fine, 4), kz, k, 4, 8, UNROLL)
    end[0] = pooled(block_sums(fine, 0, 0), pool[...])
    starts[0] = own[0]
    starts[1] = own[1]
    starts[2] = theirs[1]


def late_kernel(at, near_slow, g, a, b, kz, k, pool, fine, end, v0, c0, w0, kl, kzl):
    par = at[0]
    blank_margins(v0, 10)
    blank_margins(w0, 10)

    @pl.loop(0, 4)
    def _(i):
        put(v0, 3 - i, g[slow_plane(par, i)])
        put(c0, 3 - i, g[HALF + slow_plane(par, i)])

    for i in range(2):
        put(v0, 4 + i, near_slow[fast_plane(par, i)])
        put(c0, 4 + i, near_slow[HALF + fast_plane(par, i)])
    for i in range(6):
        mirror_margins(c0, i)
    scale = 0.5 * FINE_RATE
    fill_faces(c0, kzl, 0, 5, scale, True)
    for h in range(2):
        kzl[3, h] = jnp.where(at[1] > 0, kzl[3, h], 0.0)
    fill_coefficients(c0, kzl, kl, 1, 5, scale, True)
    advance(v0, into(w0), kzl, kl, 1, 5, True)
    for h in range(2):
        w0[5, h] = b[1, h]
        w0[6, h] = b[2, h]
    advance(w0, into(v0), kzl, kl, 2, 5, True)
    advance(w0, into(v0), kz, k, 5, 6, True, 4)
    for h in range(2):
        v0[6, h] = a[2, h]
        v0[7, h] = a[3, h]
    advance(v0, into(w0), kzl, kl, 3, 5, True)
    advance(v0, into(w0), kz, k, 5, 7, True, 4)
    for h in range(2):
        w0[7, h] = b[3, h]
        w0[8, h] = b[4, h]
    advance(w0, into_fine(fine, 4), kzl, kl, 4, 5, True)
    advance(w0, into_fine(fine, 4), kz, k, 5, 8, True, 4)
    end[0] = pooled(block_sums(fine, 0, 0), pool[...])


def row_turns(a):
    other = pltpu.roll(a, LANES // 2, 1)
    row = lax.broadcasted_iota(jnp.int32, a.shape, 0)
    up = jnp.where(row == 7, pltpu.roll(other, 7, 0), pltpu.roll(a, 7, 0))
    down = jnp.where(row == 0, pltpu.roll(other, 1, 0), pltpu.roll(a, 1, 0))
    return up, down


def weights_kernel(at, cc, kz, k):
    scale = 0.5 * COARSE_RATE
    row = lax.broadcasted_iota(jnp.int32, (8, LANES), 0)
    lane = lax.broadcasted_iota(jnp.int32, (8, LANES), 1)
    left = lane < LANES // 2
    up_ok = jnp.where(left | (row < 7), scale, 0.0)
    down_ok = jnp.where(left & (row == 0), 0.0, scale)
    right_ok = jnp.where(lane % (LANES // 2) == LANES // 2 - 1, 0.0, scale)
    left_ok = jnp.where(lane % (LANES // 2) == 0, 0.0, scale)
    faces = [(cc[i] + cc[i + 1]) * scale for i in range(7)]
    faces[2] = jnp.where(at[1] > 0, faces[2], 0.0)
    faces[6] = jnp.where(at[2] > 0, faces[6], 0.0)
    for i in range(7):
        kz[i] = faces[i]
    for i in range(6):
        c = cc[i + 1]
        up, down = row_turns(c)
        kxu, kxd = (c + up) * up_ok, (c + down) * down_ok
        kyu = (c + pltpu.roll(c, LANES - 1, 1)) * right_ok
        kyd = (c + pltpu.roll(c, 1, 1)) * left_ok
        k[i, 0] = 1.0 - ((kxu + kxd) + (kyu + kyd) + (faces[i] + faces[i + 1]))
        k[i, 1] = kxu
        k[i, 2] = kxd
        k[i, 3] = kyu
        k[i, 4] = kyd


def final_kernel(at, near, far, other, kz, k, spread, tall, lower, upper, out):
    par, slice_at = at[0], at[3]

    def pick(level, p):
        return jnp.where((par == 1) == (level == 1), near[p + 2], other[5 - p])

    def gate(level, a):
        return jnp.where(slice_at >= level, a, 0.0)

    def grow(d, lo, hi):
        u = {}
        for p in range(lo, hi):
            v = d[p]
            up, down = row_turns(v)
            w = [k[p + 2, i] for i in range(5)]
            x = w[1] * up + w[2] * down
            y = w[3] * pltpu.roll(v, LANES - 1, 1) + w[4] * pltpu.roll(v, 1, 1)
            u[p] = (w[0] * v + (kz[p + 3] * d[p + 1] + kz[p + 2] * d[p - 1])) + (x + y)
        return u

    d = {p: gate(3, jnp.where(par == 1, far[p + 3], other[14 - p])) for p in range(-3, 5)}
    u = grow(d, -2, 4)
    d = {p: u[p] + gate(2, pick(2, p)) for p in range(-2, 4)}
    u = grow(d, -1, 3)
    d = {p: u[p] + gate(1, pick(1, p)) for p in range(-1, 3)}
    u = grow(d, 0, 2)
    wide = split_dot(jnp.concatenate([u[0], u[1]], axis=0), spread[...])
    high = wide.astype(BF16)
    low = (wide - high.astype(F32)).astype(BF16)
    change = mxu(tall[...], high) + mxu(tall[...], low)
    for half, fine in ((0, lower), (1, upper)):

        @pl.loop(0, 4)
        def _(i):
            at_plane = own_plane(par, 4 * half + i)
            for side in range(2):
                for h in range(2):
                    rows = slice(32 * side, 32 * side + 32)
                    cut = change[32 * half : 32 * half + 32, 256 * side + LANES * h : 256 * side + LANES * (h + 1)]
                    out[at_plane, rows, LANES * h : LANES * (h + 1)] = fine[i, h, rows] + cut


def call(kernel, outs, scratch, flops, count):
    return pl.pallas_call(
        kernel,
        out_shape=[jax.ShapeDtypeStruct(s, F32) for s in outs],
        in_specs=[pl.BlockSpec(memory_space=pltpu.SMEM)]
        + [pl.BlockSpec(memory_space=pltpu.VMEM)] * (count - 1),
        out_specs=[pl.BlockSpec(memory_space=pltpu.VMEM)] * len(outs),
        scratch_shapes=[pltpu.VMEM(s, F32) for s in scratch],
        compiler_params=pltpu.CompilerParams(vmem_limit_bytes=VMEM_LIMIT),
        cost_estimate=pl.CostEstimate(flops=flops, bytes_accessed=flops // 4, transcendentals=0),
    )


def matches(rows, cols, by_row):
    r = lax.broadcasted_iota(jnp.int32, (rows, cols), 0)
    c = lax.broadcasted_iota(jnp.int32, (rows, cols), 1)
    return (r // COARSEN == c if by_row else c // COARSEN == r).astype(BF16)


def per_device(states, conductivity):
    return iteration(states[0], conductivity)[None]


def iteration(v, c):
    planes, rows, cols = v.shape
    plane = (rows, cols)
    wide, padded, block = (2, ROWS, LANES), (2, PADDED, LANES), (8, LANES)
    k, n = lax.axis_index("space"), lax.axis_index("tm")
    count, slices = lax.axis_size("space"), lax.axis_size("tm")
    par = k % 2
    mate = k + 1 - 2 * par
    inside = lambda i: ((i != 0) & (i != count - 1)).astype(jnp.int32)
    at = jnp.stack([par, inside(k), inside(mate), n]).astype(jnp.int32)

    slow_pairs = [(i, i + 1) for i in range(1, count - 1, 2)]
    slow_pairs += [(b, a) for a, b in slow_pairs]
    fast_pairs = [(i, i ^ 1) for i in range(count)]
    slow = lambda x: lax.ppermute(x, "space", slow_pairs)
    fast = lambda x: lax.ppermute(x, "space", fast_pairs)

    half = (2 * HALF,) + plane
    near_slow, near_fast = pl.pallas_call(
        pack_kernel,
        out_shape=[jax.ShapeDtypeStruct(half, F32)] * 2,
        in_specs=[pl.BlockSpec(memory_space=pltpu.SMEM)] + [pl.BlockSpec(memory_space=pltpu.HBM)] * 2,
        out_specs=[pl.BlockSpec(memory_space=pltpu.VMEM)] * 2,
        scratch_shapes=[pltpu.SemaphoreType.DMA((4,))],
        compiler_params=pltpu.CompilerParams(vmem_limit_bytes=PACK_LIMIT),
    )(at, *(pltpu.with_memory_space_constraint(x, pltpu.HBM) for x in (v, c)))
    from_slow = slow(near_slow)
    from_fast = fast(near_fast)
    pool = matches(512, LANES, True)
    spread = matches(LANES, 512, False)
    tall = matches(64, 16, True)

    (own,) = call(coarse_kernel, [(4,) + block], [(8,) + padded] * 2, 1_000_000, 4)(at, near_slow, near_fast, pool)
    theirs = fast(own)
    a, b, kz, kk, upper, end, starts = call(
        early_kernel,
        [(12,) + padded, (12,) + padded, (11,) + wide, (11, 5) + wide, (4,) + wide, (1,) + block, (3,) + block],
        [(12,) + padded],
        8_000_000,
        7,
    )(at, near_slow, near_fast, from_fast, pool, own, theirs)
    their_end = fast(end)
    following = lax.ppermute(starts, "tm", [(i + 1, i) for i in range(slices - 1)])
    lower, first_end = call(
        late_kernel,
        [(4,) + wide, (1,) + block],
        [(10,) + padded] * 3 + [(5, 5) + wide, (5,) + wide],
        4_000_000,
        8,
    )(at, near_slow, from_slow, a, b, kz, kk, pool)
    gaps = jnp.concatenate([first_end, end, their_end]) - following
    beyond = slow(jnp.concatenate([gaps, own[2:], theirs[3:]]))
    late = fast(jnp.concatenate([gaps[:1], beyond[:4]]))

    line = jnp.stack(
        [beyond[2], beyond[1], beyond[0], gaps[0], gaps[1], gaps[2], late[0], late[1], late[2], late[3]]
    )
    pairs = []
    for i in range(count):
        step = 2 - i % 2
        pairs += [(s * count + i, (s + step) * count + i) for s in range(slices - step)]
    near = lax.ppermute(line[1:9], ("tm", "space"), pairs)
    far = lax.ppermute(line, ("tm", "space"), [(i, (slices - 1) * count + i) for i in range(1, count, 2)])
    cc = jnp.stack([beyond[5], beyond[4], beyond[3], own[2], own[3], theirs[3], theirs[2], late[4]])
    ckz, ck = call(weights_kernel, [(7,) + block, (6, 5) + block], [], 100_000, 2)(at, cc)
    other = fast(jnp.concatenate([near, far]))
    (result,) = call(final_kernel, [(planes,) + plane], [], 1_000_000, 10)(
        at, near, far, other, ckz, ck, spread, tall, lower, upper
    )
    return result


def solution(mesh):
    return jax.shard_map(
        per_device,
        mesh=mesh,
        in_specs=(P("tm", "space", None, None), P("space", None, None)),
        out_specs=P("tm", "space", None, None),
        check_vma=False,
    )
```

time: 53.8 us -> 45.7 us (0.85)
  the two profiles are of different devices: /device:TPU:7 before, /device:TPU:161 now
where the time goes in v2:
time: 45.7 us; the launch traced here: 45.4 us
  starting transfers between devices  24.9 us (54%)
  waiting for transfers between devices  10.1 us (22%)
  Pallas kernels  9.74 us (21%)
  other arithmetic  0.52 us (1%)
    ppermute x5, starting transfers between devices, iteration(): fast = lambda x: lax.ppermute(x, 'space', fast_pairs)  15.2 us
    ppermute x2, starting transfers between devices, iteration(): slow = lambda x: lax.ppermute(x, 'space', slow_pairs)  5.02 us
    ppermute x1, waiting for transfers between devices, iteration(): near = lax.ppermute(line[1:9], ('tm', 'space'), pairs)  4.04 us
    ppermute x2, waiting for transfers between devices, iteration(): slow = lambda x: lax.ppermute(x, 'space', slow_pairs)  3.2 us
    pallas_call x1, Pallas kernels, iteration(): call(early_kernel, [(12,) + padded, (12,) + padded, (11,) + wide, (11, 5)...  2.72 us
    ppermute x1, starting transfers between devices, iteration(): near = lax.ppermute(line[1:9], ('tm', 'space'), pairs)  2.02 us
    pallas_call x1, Pallas kernels, iteration(): call(final_kernel, [(planes,) + plane], [], 1000000, 10)  1.93 us
    ppermute x1, starting transfers between devices, iteration(): lax.ppermute(starts, 'tm', [(i + 1, i) for i in range(slices - 1)])  1.93 us
  transfers between devices with their start and end apart: 10, of which 6 were waited for; matrix products, arithmetic and copies ran while one was open for 1% of the time, Pallas kernels for 13%

profile of v2, /device:TPU:161, one launch (start us, length us, event | category | flops | bytes accessed | tf_op | source)
XLA Modules:
  0.0 45.4 jit_solution(14357139148920701057)
XLA Ops:
  0.0 0.1 pad_add_fusion.at
  0.1 1.8 %shard_map.28 = (f32[8,64,256]{2,1,0:T(8,128)S(1)}, f32[8,64,256]{2,1,0:T(8,128)S(1)}) custom-call(s32[4]{0:T(128)S(1)} %pad_add_fusion.at, f32[8,64,256]{2,1,0:T(8,128)} %bitcast.6, f32[8,64,256]{2,1,0:T(8,128)} %c.1), custom_call_target="tpu_custom_call" | custom-call | tf_op jit(solution)/shard_map/pallas_call | solution.py:377
  1.9 0.8 %collective-permute-start.1 = (f32[8,64,256]{2,1,0:T(8,128)S(1)}, f32[8,64,256]{2,1,0:T(8,128)S(1)}, u32[]{:S(2)}, u32[]{:S(2)}) collective-permute-start(f32[8,64,256]{2,1,0:T(8,128)S(1)} %get-tuple-element.19.near_fast), channel_id=1, source_target_pairs={{0,1},{1,0},{2,3},{3,2},{4,5},{5,4},{6,7},{7,6},{8,9},{9,8},{10,11... | collective-permute-start | bytes 1572872 | tf_op jit(solution)/shard_map/ppermute | solution.py:374
  2.6 3.1 %collective-permute-start = (f32[8,64,256]{2,1,0:T(8,128)S(1)}, f32[8,64,256]{2,1,0:T(8,128)S(1)}, u32[]{:S(2)}, u32[]{:S(2)}) collective-permute-start(f32[8,64,256]{2,1,0:T(8,128)S(1)} %get-tuple-element.18.near_slow), channel_id=1, source_target_pairs={{1,2},{3,4},{5,6},{7,8},{9,10},{11,12},{13,14},{15,16},{17,18},{19... | collective-permute-start | bytes 1572872 | tf_op jit(solution)/shard_map/ppermute | solution.py:373
  5.7 0.3 fusion.pool
  6.0 0.8 %shard_map.29.own = f32[4,8,128]{2,1,0:T(8,128)S(1)} custom-call(s32[4]{0:T(128)S(1)} %pad_add_fusion.at, f32[8,64,256]{2,1,0:T(8,128)S(1)} %get-tuple-element.18.near_slow, f32[8,64,256]{2,1,0:T(8,128)S(1)} %get-tuple-element.19.near_fast, bf16[512,128]{1,0:T(8,128)(2,1)S(1)} %fusion.pool), custom_call_target="tpu_custom_call" | custom-call | flops 1000000 | bytes 250000 | tf_op jit(solution)/shard_map/pallas_call | solution.py:391
  6.9 4.6 %collective-permute-start.2 = (f32[4,8,128]{2,1,0:T(8,128)S(1)}, f32[4,8,128]{2,1,0:T(8,128)S(1)}, u32[]{:S(2)}, u32[]{:S(2)}) collective-permute-start(f32[4,8,128]{2,1,0:T(8,128)S(1)} %shard_map.29.own), channel_id=1, source_target_pairs={{0,1},{1,0},{2,3},{3,2},{4,5},{5,4},{6,7},{7,6},{8,9},{9,8},{10,11... | collective-permute-start | bytes 49160 | tf_op jit(solution)/shard_map/ppermute | solution.py:374
  11.5 0.8 %collective-permute-done.2.theirs = f32[4,8,128]{2,1,0:T(8,128)S(1)} collective-permute-done((f32[4,8,128]{2,1,0:T(8,128)S(1)}, f32[4,8,128]{2,1,0:T(8,128)S(1)}, u32[]{:S(2)}, u32[]{:S(2)}) %collective-permute-start.2) | collective-permute-done | bytes 16416 | tf_op jit(solution)/shard_map/ppermute | solution.py:374
  12.3 0.0 collective-permute-done.1.h
  12.3 2.7 %shard_map.30 = (f32[12,2,80,128]{3,2,1,0:T(8,128)S(1)}, f32[12,2,80,128]{3,2,1,0:T(8,128)S(1)}, f32[11,2,64,128]{3,2,1,0:T(8,128)S(1)}, f32[11,5,2,64,128]{4,3,...) custom-call(s32[4]{0:T(128)S(1)} %pad_add_fusion.at, ...), custom_call_target="tpu_custom_call" | custom-call | flops 8000000 | bytes 2000000 | tf_op jit(solution)/shard_map/pallas_call | solution.py:393
  15.1 1.9 %collective-permute-start.4 = (f32[3,8,128]{2,1,0:T(8,128)S(1)}, f32[3,8,128]{2,1,0:T(8,128)S(1)}, u32[]{:S(2)}, u32[]{:S(2)}) collective-permute-start(f32[3,8,128]{2,1,0:T(8,128)S(1)} %get-tuple-element.26), channel_id=1, source_target_pairs={{64,0},{128,64},{192,128},{65,1},{129,65},{193,129},{66,2},{130,66... | collective-permute-start | bytes 36872 | tf_op jit(solution)/shard_map/ppermute | solution.py:401
  17.0 0.4 collective-permute-start.3
  17.4 0.0 collective-permute-done.g
  17.4 1.9 %shard_map.31 = (f32[4,2,64,128]{3,2,1,0:T(8,128)S(1)}, f32[1,8,128]{2,1,0:T(8,128)S(1)}) custom-call(s32[4]{0:T(128)S(1)} %pad_add_fusion.at, f32[8,64,256]{2,1,0:T(8,128)S(1)} %get-tuple-element.18.near_slow, f32[8,64,256]{2,1,0:T(8,128)S(1)} %collective-permute-done.g, f32[12,2,80,128]{3,2,1,0:T(8,128)S(1)} %get-tuple-element.20.a, ...), custom_call_target="tpu_custom_call" | custom-call | flops 4000000 | bytes 1000000 | tf_op jit(solution)/shard_map/pallas_call | solution.py:402
  19.3 0.0 collective-permute-done.3
  19.3 1.1 %collective-permute-done.4 = f32[3,8,128]{2,1,0:T(8,128)S(1)} collective-permute-done((f32[3,8,128]{2,1,0:T(8,128)S(1)}, f32[3,8,128]{2,1,0:T(8,128)S(1)}, u32[]{:S(2)}, u32[]{:S(2)}) %collective-permute-start.4) | collective-permute-done | bytes 12320 | tf_op jit(solution)/shard_map/ppermute | solution.py:401
  20.4 1.9 %collective-permute-start.5 = (f32[6,8,128]{2,1,0:T(8,128)S(1)}, f32[6,8,128]{2,1,0:T(8,128)S(1)}, u32[]{:S(2)}, u32[]{:S(2)}) collective-permute-start(f32[6,8,128]{2,1,0:T(8,128)S(1)} %pad_maximum_fusion.4), channel_id=1, source_target_pairs={{1,2},{3,4},{5,6},{7,8},{9,10},{11,12},{13,14},{15,16},{17,18},{19... | collective-permute-start | bytes 73736 | tf_op jit(solution)/shard_map/ppermute | solution.py:373
  22.4 3.2 %collective-permute-done.5 = f32[6,8,128]{2,1,0:T(8,128)S(1)} collective-permute-done((f32[6,8,128]{2,1,0:T(8,128)S(1)}, f32[6,8,128]{2,1,0:T(8,128)S(1)}, u32[]{:S(2)}, u32[]{:S(2)}) %collective-permute-start.5) | collective-permute-done | bytes 24608 | tf_op jit(solution)/shard_map/ppermute | solution.py:373
  25.6 5.8 %collective-permute-start.6 = (f32[5,8,128]{2,1,0:T(8,128)S(1)}, f32[5,8,128]{2,1,0:T(8,128)S(1)}, u32[]{:S(2)}, u32[]{:S(2)}) collective-permute-start(f32[5,8,128]{2,1,0:T(8,128)S(1)} %pad_maximum_fusion.5), channel_id=1, source_target_pairs={{0,1},{1,0},{2,3},{3,2},{4,5},{5,4},{6,7},{7,6},{8,9},{9,8},{10,11... | collective-permute-start | bytes 61448 | tf_op jit(solution)/shard_map/ppermute | solution.py:374
  31.4 0.8 %collective-permute-done.6 = f32[5,8,128]{2,1,0:T(8,128)S(1)} collective-permute-done((f32[5,8,128]{2,1,0:T(8,128)S(1)}, f32[5,8,128]{2,1,0:T(8,128)S(1)}, u32[]{:S(2)}, u32[]{:S(2)}) %collective-permute-start.6) | collective-permute-done | bytes 20512 | tf_op jit(solution)/shard_map/ppermute | solution.py:374
  32.3 2.0 %collective-permute-start.7 = (f32[8,8,128]{2,1,0:T(8,128)S(1)}, f32[8,8,128]{2,1,0:T(8,128)S(1)}, u32[]{:S(2)}, u32[]{:S(2)}) collective-permute-start(f32[8,8,128]{2,1,0:T(8,128)S(1)} %pad_maximum_fusion.1), channel_id=1, source_target_pairs={{0,128},{64,192},{1,65},{65,129},{129,193},{2,130},{66,194},{3,67}... | collective-permute-start | bytes 98312 | tf_op jit(solution)/shard_map/ppermute | solution.py:420
  34.3 0.7 %collective-permute-start.8 = (f32[10,8,128]{2,1,0:T(8,128)S(1)}, f32[10,8,128]{2,1,0:T(8,128)S(1)}, u32[]{:S(2)}, u32[]{:S(2)}) collective-permute-start(f32[10,8,128]{2,1,0:T(8,128)S(1)} %get-tuple-element.37), channel_id=1, source_target_pairs={{1,193},{3,195},{5,197},{7,199},{9,201},{11,203},{13,205},{15,207}... | collective-permute-start | bytes 122888 | tf_op jit(solution)/shard_map/ppermute | solution.py:421
  35.0 4.0 %collective-permute-done.7.near = f32[8,8,128]{2,1,0:T(8,128)S(1)} collective-permute-done((f32[8,8,128]{2,1,0:T(8,128)S(1)}, f32[8,8,128]{2,1,0:T(8,128)S(1)}, u32[]{:S(2)}, u32[]{:S(2)}) %collective-permute-start.7) | collective-permute-done | bytes 32800 | tf_op jit(solution)/shard_map/ppermute | solution.py:420
  39.0 0.0 collective-permute-done.8.far
  39.0 3.6 %collective-permute-start.9 = (f32[18,8,128]{2,1,0:T(8,128)S(1)}, f32[18,8,128]{2,1,0:T(8,128)S(1)}, u32[]{:S(2)}, u32[]{:S(2)}) collective-permute-start(f32[18,8,128]{2,1,0:T(8,128)S(1)} %pad_maximum_fusion), channel_id=1, source_target_pairs={{0,1},{1,0},{2,3},{3,2},{4,5},{5,4},{6,7},{7,6},{8,9},{9,8},{10,11... | collective-permute-start | bytes 221192 | tf_op jit(solution)/shard_map/ppermute | solution.py:374
  42.6 0.1 fusion.2.tall
  42.7 0.6 %shard_map.32 = (f32[7,8,128]{2,1,0:T(8,128)S(1)}, f32[6,5,8,128]{3,2,1,0:T(8,128)S(1)}) custom-call(s32[4]{0:T(128)S(1)} %pad_add_fusion.at, f32[8,8,128]{2,1,0:T(8,128)S(1)} %constant_dynamic-update-slice_fusion.5.cc), custom_call_target="tpu_custom_call" | custom-call | flops 100000 | bytes 25000 | tf_op jit(solution)/shard_map/pallas_call | solution.py:423
  43.3 0.2 collective-permute-done.9.other
  43.5 1.9 %shard_map.33 = f32[8,64,256]{2,1,0:T(8,128)} custom-call(s32[4]{0:T(128)S(1)} %pad_add_fusion.at, f32[8,8,128]{2,1,0:T(8,128)S(1)} %collective-permute-done.7.near, f32[10,8,128]{2,1,0:T(8,128)S(1)} %collective-permute-done.8.far, f32[18,8,128]{2,1,0:T(8,128)S(1)} %collective-permute-done.9.other, f32[7,8,128]{2,1,0:T(8,128)S(1)} %get-tuple-element.27.kz, ...), custom_call_target="tpu_custom_call" | custom-call | flops 1000000 | bytes 250000 | tf_op jit(solution)/shard_map/pallas_call | solution.py:425
  (24 shorter events, 0.1 us)
Async XLA Ops:
  1.9 10.5 %collective-permute-start.1 = (f32[8,64,256]{2,1,0:T(8,128)S(1)}, f32[8,64,256]{2,1,0:T(8,128)S(1)}, u32[]{:S(2)}, u32[]{:S(2)}) collective-permute-start(f32[8,64,256]{2,1,0:T(8,128)S(1)} %get-tuple-element.19.near_fast), channel_id=1, source_target_pairs={{0,1},{1,0},{2,3},{3,2},{4,5},{5,4},{6,7},{7,6},{8,9},{9,8},{10,11... | collective-permute-start | bytes 1572872 | tf_op jit(solution)/shard_map/ppermute | solution.py:374
  2.6 14.8 %collective-permute-start = (f32[8,64,256]{2,1,0:T(8,128)S(1)}, f32[8,64,256]{2,1,0:T(8,128)S(1)}, u32[]{:S(2)}, u32[]{:S(2)}) collective-permute-start(f32[8,64,256]{2,1,0:T(8,128)S(1)} %get-tuple-element.18.near_slow), channel_id=1, source_target_pairs={{1,2},{3,4},{5,6},{7,8},{9,10},{11,12},{13,14},{15,16},{17,18},{19... | collective-permute-start | bytes 1572872 | tf_op jit(solution)/shard_map/ppermute | solution.py:373
  6.9 5.5 %collective-permute-start.2 = (f32[4,8,128]{2,1,0:T(8,128)S(1)}, f32[4,8,128]{2,1,0:T(8,128)S(1)}, u32[]{:S(2)}, u32[]{:S(2)}) collective-permute-start(f32[4,8,128]{2,1,0:T(8,128)S(1)} %shard_map.29.own), channel_id=1, source_target_pairs={{0,1},{1,0},{2,3},{3,2},{4,5},{5,4},{6,7},{7,6},{8,9},{9,8},{10,11... | collective-permute-start | bytes 49160 | tf_op jit(solution)/shard_map/ppermute | solution.py:374
  15.1 5.3 %collective-permute-start.4 = (f32[3,8,128]{2,1,0:T(8,128)S(1)}, f32[3,8,128]{2,1,0:T(8,128)S(1)}, u32[]{:S(2)}, u32[]{:S(2)}) collective-permute-start(f32[3,8,128]{2,1,0:T(8,128)S(1)} %get-tuple-element.26), channel_id=1, source_target_pairs={{64,0},{128,64},{192,128},{65,1},{129,65},{193,129},{66,2},{130,66... | collective-permute-start | bytes 36872 | tf_op jit(solution)/shard_map/ppermute | solution.py:401
  17.0 2.3 %collective-permute-start.3 = (f32[1,8,128]{2,1,0:T(8,128)S(1)}, f32[1,8,128]{2,1,0:T(8,128)S(1)}, u32[]{:S(2)}, u32[]{:S(2)}) collective-permute-start(f32[1,8,128]{2,1,0:T(8,128)S(1)} %get-tuple-element.25), channel_id=1, source_target_pairs={{0,1},{1,0},{2,3},{3,2},{4,5},{5,4},{6,7},{7,6},{8,9},{9,8},{10,11... | collective-permute-start | bytes 12296 | tf_op jit(solution)/shard_map/ppermute | solution.py:374
  20.4 5.1 %collective-permute-start.5 = (f32[6,8,128]{2,1,0:T(8,128)S(1)}, f32[6,8,128]{2,1,0:T(8,128)S(1)}, u32[]{:S(2)}, u32[]{:S(2)}) collective-permute-start(f32[6,8,128]{2,1,0:T(8,128)S(1)} %pad_maximum_fusion.4), channel_id=1, source_target_pairs={{1,2},{3,4},{5,6},{7,8},{9,10},{11,12},{13,14},{15,16},{17,18},{19... | collective-permute-start | bytes 73736 | tf_op jit(solution)/shard_map/ppermute | solution.py:373
  25.6 6.6 %collective-permute-start.6 = (f32[5,8,128]{2,1,0:T(8,128)S(1)}, f32[5,8,128]{2,1,0:T(8,128)S(1)}, u32[]{:S(2)}, u32[]{:S(2)}) collective-permute-start(f32[5,8,128]{2,1,0:T(8,128)S(1)} %pad_maximum_fusion.5), channel_id=1, source_target_pairs={{0,1},{1,0},{2,3},{3,2},{4,5},{5,4},{6,7},{7,6},{8,9},{9,8},{10,11... | collective-permute-start | bytes 61448 | tf_op jit(solution)/shard_map/ppermute | solution.py:374
  32.3 6.8 %collective-permute-start.7 = (f32[8,8,128]{2,1,0:T(8,128)S(1)}, f32[8,8,128]{2,1,0:T(8,128)S(1)}, u32[]{:S(2)}, u32[]{:S(2)}) collective-permute-start(f32[8,8,128]{2,1,0:T(8,128)S(1)} %pad_maximum_fusion.1), channel_id=1, source_target_pairs={{0,128},{64,192},{1,65},{65,129},{129,193},{2,130},{66,194},{3,67}... | collective-permute-start | bytes 98312 | tf_op jit(solution)/shard_map/ppermute | solution.py:420
  34.3 4.7 %collective-permute-start.8 = (f32[10,8,128]{2,1,0:T(8,128)S(1)}, f32[10,8,128]{2,1,0:T(8,128)S(1)}, u32[]{:S(2)}, u32[]{:S(2)}) collective-permute-start(f32[10,8,128]{2,1,0:T(8,128)S(1)} %get-tuple-element.37), channel_id=1, source_target_pairs={{1,193},{3,195},{5,197},{7,199},{9,201},{11,203},{13,205},{15,207}... | collective-permute-start | bytes 122888 | tf_op jit(solution)/shard_map/ppermute | solution.py:421
  39.0 4.5 %collective-permute-start.9 = (f32[18,8,128]{2,1,0:T(8,128)S(1)}, f32[18,8,128]{2,1,0:T(8,128)S(1)}, u32[]{:S(2)}, u32[]{:S(2)}) collective-permute-start(f32[18,8,128]{2,1,0:T(8,128)S(1)} %pad_maximum_fusion), channel_id=1, source_target_pairs={{0,1},{1,0},{2,3},{3,2},{4,5},{5,4},{6,7},{7,6},{8,9},{9,8},{10,11... | collective-permute-start | bytes 221192 | tf_op jit(solution)/shard_map/ppermute | solution.py:374

commit v3 on v2

--- a/solution.py
+++ b/solution.py
@@ -14,17 +14,12 @@
 F32 = jnp.float32
 BF16 = jnp.bfloat16
 VMEM_LIMIT = 24 * 1024 * 1024
-PACK_LIMIT = VMEM_LIMIT
 LANES = 128
 ROWS = 64
 TOP = 8
 PADDED = 80
 UNROLL = True
 CHUNK = 8
-
-
-def own_plane(par, i):
-    return i + par * (7 - 2 * i)
 
 
 def fast_plane(par, i):
@@ -159,7 +154,14 @@
     return split_dot(sums, pool) * (1.0 / COARSEN**3)
 
 
-def pack_kernel(at, v, c, near_slow, near_fast, sems):
+def matches(rows, cols, by_row):
+    r = lax.broadcasted_iota(jnp.int32, (rows, cols), 0)
+    c = lax.broadcasted_iota(jnp.int32, (rows, cols), 1)
+    same = r // COARSEN == c if by_row else c // COARSEN == r
+    return jnp.where(same, 1.0, 0.0).astype(BF16)
+
+
+def pack_kernel(at, v, c, near_slow, near_fast, pool, spread, tall, sems):
     par = at[0]
     copies = []
     for s, (ref, side) in enumerate(((near_slow, par), (near_fast, 1 - par))):
@@ -171,6 +173,9 @@
             )
     for copy in copies:
         copy.start()
+    pool[...] = matches(*pool.shape, True)
+    spread[...] = matches(*spread.shape, False)
+    tall[...] = matches(*tall.shape, True)
     for copy in copies:
         copy.wait()
 
@@ -191,7 +196,7 @@
         out[i] = res[8 * i : 8 * i + 8]
 
 
-def early_kernel(at, near_slow, near_fast, h, pool, own, theirs, a, b, kz, k, fine, end, starts, c0):
+def early_kernel(at, near_slow, near_fast, h, pool, a, b, kz, k, fine, end, c0):
     par = at[0]
     blank_margins(a, 12)
     blank_margins(b, 12)
@@ -212,48 +217,6 @@
     advance(a, into(b), kz, k, 3, 9, UNROLL)
     advance(b, into_fine(fine, 4), kz, k, 4, 8, UNROLL)
     end[0] = pooled(block_sums(fine, 0, 0), pool[...])
-    starts[0] = own[0]
-    starts[1] = own[1]
-    starts[2] = theirs[1]
-
-
-def late_kernel(at, near_slow, g, a, b, kz, k, pool, fine, end, v0, c0, w0, kl, kzl):
-    par = at[0]
-    blank_margins(v0, 10)
-    blank_margins(w0, 10)
-
-    @pl.loop(0, 4)
-    def _(i):
-        put(v0, 3 - i, g[slow_plane(par, i)])
-        put(c0, 3 - i, g[HALF + slow_plane(par, i)])
-
-    for i in range(2):
-        put(v0, 4 + i, near_slow[fast_plane(par, i)])
-        put(c0, 4 + i, near_slow[HALF + fast_plane(par, i)])
-    for i in range(6):
-        mirror_margins(c0, i)
-    scale = 0.5 * FINE_RATE
-    fill_faces(c0, kzl, 0, 5, scale, True)
-    for h in range(2):
-        kzl[3, h] = jnp.where(at[1] > 0, kzl[3, h], 0.0)
-    fill_coefficients(c0, kzl, kl, 1, 5, scale, True)
-    advance(v0, into(w0), kzl, kl, 1, 5, True)
-    for h in range(2):
-        w0[5, h] = b[1, h]
-        w0[6, h] = b[2, h]
-    advance(w0, into(v0), kzl, kl, 2, 5, True)
-    advance(w0, into(v0), kz, k, 5, 6, True, 4)
-    for h in range(2):
-        v0[6, h] = a[2, h]
-        v0[7, h] = a[3, h]
-    advance(v0, into(w0), kzl, kl, 3, 5, True)
-    advance(v0, into(w0), kz, k, 5, 7, True, 4)
-    for h in range(2):
-        w0[7, h] = b[3, h]
-        w0[8, h] = b[4, h]
-    advance(w0, into_fine(fine, 4), kzl, kl, 4, 5, True)
-    advance(w0, into_fine(fine, 4), kz, k, 5, 8, True, 4)
-    end[0] = pooled(block_sums(fine, 0, 0), pool[...])
 
 
 def row_turns(a):
@@ -264,34 +227,102 @@
     return up, down
 
 
-def weights_kernel(at, cc, kz, k):
+def coarse_masks():
     scale = 0.5 * COARSE_RATE
     row = lax.broadcasted_iota(jnp.int32, (8, LANES), 0)
     lane = lax.broadcasted_iota(jnp.int32, (8, LANES), 1)
     left = lane < LANES // 2
-    up_ok = jnp.where(left | (row < 7), scale, 0.0)
-    down_ok = jnp.where(left & (row == 0), 0.0, scale)
-    right_ok = jnp.where(lane % (LANES // 2) == LANES // 2 - 1, 0.0, scale)
-    left_ok = jnp.where(lane % (LANES // 2) == 0, 0.0, scale)
-    faces = [(cc[i] + cc[i + 1]) * scale for i in range(7)]
+    up = jnp.where(left | (row < 7), scale, 0.0)
+    down = jnp.where(left & (row == 0), 0.0, scale)
+    right = jnp.where(lane % (LANES // 2) == LANES // 2 - 1, 0.0, scale)
+    before = jnp.where(lane % (LANES // 2) == 0, 0.0, scale)
+    return up, down, right, before
+
+
+def coarse_weights(c, faces, masks):
+    up, down = row_turns(c)
+    kxu, kxd = (c + up) * masks[0], (c + down) * masks[1]
+    kyu = (c + pltpu.roll(c, LANES - 1, 1)) * masks[2]
+    kyd = (c + pltpu.roll(c, 1, 1)) * masks[3]
+    return 1.0 - ((kxu + kxd) + (kyu + kyd) + faces), kxu, kxd, kyu, kyd
+
+
+def coarse_step(v, above, below, face_above, face_below, w):
+    up, down = row_turns(v)
+    x = w[1] * up + w[2] * down
+    y = w[3] * pltpu.roll(v, LANES - 1, 1) + w[4] * pltpu.roll(v, 1, 1)
+    return (w[0] * v + (face_above * above + face_below * below)) + (x + y)
+
+
+def late_kernel(
+    at, near_slow, g, a, b, kz, k, pool, own, theirs, end, mate_end, fine, out, before, v0, c0, w0, kl, kzl
+):
+    par = at[0]
+    blank_margins(v0, 10)
+    blank_margins(w0, 10)
+
+    @pl.loop(0, 4)
+    def _(i):
+        put(v0, 3 - i, g[slow_plane(par, i)])
+        put(c0, 3 - i, g[HALF + slow_plane(par, i)])
+
+    for i in range(2):
+        put(v0, 4 + i, near_slow[fast_plane(par, i)])
+        put(c0, 4 + i, near_slow[HALF + fast_plane(par, i)])
+    for i in range(6):
+        mirror_margins(c0, i)
+    beyond = pooled(jnp.concatenate([block_sums(v0, 0, TOP), block_sums(c0, 0, TOP)], axis=0), pool[...])
+    start = [beyond[:8], own[0], own[1], theirs[1], theirs[0]]
+    cc = [beyond[8:], own[2], own[3], theirs[3], theirs[2]]
+    faces = [(cc[i] + cc[i + 1]) * (0.5 * COARSE_RATE) for i in range(4)]
+    faces[0] = jnp.where(at[1] > 0, faces[0], 0.0)
+    masks = coarse_masks()
+    before[0] = start[0]
+    stepped = []
+    for i in range(1, 4):
+        w = coarse_weights(cc[i], faces[i] + faces[i - 1], masks)
+        step = coarse_step(start[i], start[i + 1], start[i - 1], faces[i], faces[i - 1], w)
+        stepped.append(jnp.where(at[3] > 0, step, 0.0))
+        out[2 + i] = cc[i]
+    out[1] = end[0] - stepped[1]
+    out[2] = mate_end[0] - stepped[2]
+    scale = 0.5 * FINE_RATE
+    fill_faces(c0, kzl, 0, 5, scale, True)
+    for h in range(2):
+        kzl[3, h] = jnp.where(at[1] > 0, kzl[3, h], 0.0)
+    fill_coefficients(c0, kzl, kl, 1, 5, scale, True)
+    advance(v0, into(w0), kzl, kl, 1, 5, True)
+    for h in range(2):
+        w0[5, h] = b[1, h]
+        w0[6, h] = b[2, h]
+    advance(w0, into(v0), kzl, kl, 2, 5, True)
+    advance(w0, into(v0), kz, k, 5, 6, True, 4)
+    for h in range(2):
+        v0[6, h] = a[2, h]
+        v0[7, h] = a[3, h]
+    advance(v0, into(w0), kzl, kl, 3, 5, True)
+    advance(v0, into(w0), kz, k, 5, 7, True, 4)
+    for h in range(2):
+        w0[7, h] = b[3, h]
+        w0[8, h] = b[4, h]
+    advance(w0, into_fine(fine, 4), kzl, kl, 4, 5, True)
+    advance(w0, into_fine(fine, 4), kz, k, 5, 8, True, 4)
+    out[0] = pooled(block_sums(fine, 0, 0), pool[...]) - stepped[0]
+
+
+def weights_kernel(at, cc, kz, k):
+    masks = coarse_masks()
+    faces = [(cc[i] + cc[i + 1]) * (0.5 * COARSE_RATE) for i in range(7)]
     faces[2] = jnp.where(at[1] > 0, faces[2], 0.0)
     faces[6] = jnp.where(at[2] > 0, faces[6], 0.0)
     for i in range(7):
         kz[i] = faces[i]
     for i in range(6):
-        c = cc[i + 1]
-        up, down = row_turns(c)
-        kxu, kxd = (c + up) * up_ok, (c + down) * down_ok
-        kyu = (c + pltpu.roll(c, LANES - 1, 1)) * right_ok
-        kyd = (c + pltpu.roll(c, 1, 1)) * left_ok
-        k[i, 0] = 1.0 - ((kxu + kxd) + (kyu + kyd) + (faces[i] + faces[i + 1]))
-        k[i, 1] = kxu
-        k[i, 2] = kxd
-        k[i, 3] = kyu
-        k[i, 4] = kyd
-
-
-def final_kernel(at, near, far, other, kz, k, spread, tall, lower, upper, out):
+        for f, a in enumerate(coarse_weights(cc[i + 1], faces[i] + faces[i + 1], masks)):
+            k[i, f] = a
+
+
+def final_kernel(at, near, far, other, own_start, kz, k, spread, tall, lower, upper, out, made, sems):
     par, slice_at = at[0], at[3]
 
     def pick(level, p):
@@ -301,36 +332,37 @@
         return jnp.where(slice_at >= level, a, 0.0)
 
     def grow(d, lo, hi):
-        u = {}
-        for p in range(lo, hi):
-            v = d[p]
-            up, down = row_turns(v)
-            w = [k[p + 2, i] for i in range(5)]
-            x = w[1] * up + w[2] * down
-            y = w[3] * pltpu.roll(v, LANES - 1, 1) + w[4] * pltpu.roll(v, 1, 1)
-            u[p] = (w[0] * v + (kz[p + 3] * d[p + 1] + kz[p + 2] * d[p - 1])) + (x + y)
-        return u
+        return {
+            p: coarse_step(d[p], d[p + 1], d[p - 1], kz[p + 3], kz[p + 2], [k[p + 2, i] for i in range(5)])
+            for p in range(lo, hi)
+        }
 
     d = {p: gate(3, jnp.where(par == 1, far[p + 3], other[14 - p])) for p in range(-3, 5)}
     u = grow(d, -2, 4)
     d = {p: u[p] + gate(2, pick(2, p)) for p in range(-2, 4)}
     u = grow(d, -1, 3)
-    d = {p: u[p] + gate(1, pick(1, p)) for p in range(-1, 3)}
+    d = {p: gate(1, u[p] + pick(1, p) - own_start[p + 1]) for p in range(-1, 3)}
     u = grow(d, 0, 2)
     wide = split_dot(jnp.concatenate([u[0], u[1]], axis=0), spread[...])
     high = wide.astype(BF16)
     low = (wide - high.astype(F32)).astype(BF16)
     change = mxu(tall[...], high) + mxu(tall[...], low)
+    copies = []
     for half, fine in ((0, lower), (1, upper)):
 
         @pl.loop(0, 4)
         def _(i):
-            at_plane = own_plane(par, 4 * half + i)
             for side in range(2):
                 for h in range(2):
                     rows = slice(32 * side, 32 * side + 32)
                     cut = change[32 * half : 32 * half + 32, 256 * side + LANES * h : 256 * side + LANES * (h + 1)]
-                    out[at_plane, rows, LANES * h : LANES * (h + 1)] = fine[i, h, rows] + cut
+                    made[half, fast_plane(par, i), rows, LANES * h : LANES * (h + 1)] = fine[i, h, rows] + cut
+
+        first = HALF * (par if half == 0 else 1 - par)
+        copies.append(pltpu.make_async_copy(made.at[half], out.at[pl.ds(first, HALF)], sems.at[half]))
+        copies[-1].start()
+    for copy in copies:
+        copy.wait()
 
 
 def call(kernel, outs, scratch, flops, count):
@@ -346,12 +378,6 @@
     )
 
 
-def matches(rows, cols, by_row):
-    r = lax.broadcasted_iota(jnp.int32, (rows, cols), 0)
-    c = lax.broadcasted_iota(jnp.int32, (rows, cols), 1)
-    return (r // COARSEN == c if by_row else c // COARSEN == r).astype(BF16)
-
-
 def per_device(states, conductivity):
     return iteration(states[0], conductivity)[None]
 
@@ -374,44 +400,40 @@
     fast = lambda x: lax.ppermute(x, "space", fast_pairs)
 
     half = (2 * HALF,) + plane
-    near_slow, near_fast = pl.pallas_call(
+    near_slow, near_fast, pool, spread, tall = pl.pallas_call(
         pack_kernel,
-        out_shape=[jax.ShapeDtypeStruct(half, F32)] * 2,
+        out_shape=[jax.ShapeDtypeStruct(half, F32)] * 2
+        + [jax.ShapeDtypeStruct(m, BF16) for m in ((512, LANES), (LANES, 512), (64, 16))],
         in_specs=[pl.BlockSpec(memory_space=pltpu.SMEM)] + [pl.BlockSpec(memory_space=pltpu.HBM)] * 2,
-        out_specs=[pl.BlockSpec(memory_space=pltpu.VMEM)] * 2,
+        out_specs=[pl.BlockSpec(memory_space=pltpu.VMEM)] * 5,
         scratch_shapes=[pltpu.SemaphoreType.DMA((4,))],
-        compiler_params=pltpu.CompilerParams(vmem_limit_bytes=PACK_LIMIT),
+        compiler_params=pltpu.CompilerParams(vmem_limit_bytes=VMEM_LIMIT),
     )(at, *(pltpu.with_memory_space_constraint(x, pltpu.HBM) for x in (v, c)))
     from_slow = slow(near_slow)
     from_fast = fast(near_fast)
-    pool = matches(512, LANES, True)
-    spread = matches(LANES, 512, False)
-    tall = matches(64, 16, True)
 
     (own,) = call(coarse_kernel, [(4,) + block], [(8,) + padded] * 2, 1_000_000, 4)(at, near_slow, near_fast, pool)
     theirs = fast(own)
-    a, b, kz, kk, upper, end, starts = call(
+    a, b, kz, kk, upper, end = call(
         early_kernel,
-        [(12,) + padded, (12,) + padded, (11,) + wide, (11, 5) + wide, (4,) + wide, (1,) + block, (3,) + block],
+        [(12,) + padded, (12,) + padded, (11,) + wide, (11, 5) + wide, (4,) + wide, (1,) + block],
         [(12,) + padded],
         8_000_000,
-        7,
-    )(at, near_slow, near_fast, from_fast, pool, own, theirs)
-    their_end = fast(end)
-    following = lax.ppermute(starts, "tm", [(i + 1, i) for i in range(slices - 1)])
-    lower, first_end = call(
+        5,
+    )(at, near_slow, near_fast, from_fast, pool)
+    mate_end = fast(end)
+    lower, first, before = call(
         late_kernel,
-        [(4,) + wide, (1,) + block],
+        [(4,) + wide, (6,) + block, (1,) + block],
         [(10,) + padded] * 3 + [(5, 5) + wide, (5,) + wide],
         4_000_000,
-        8,
-    )(at, near_slow, from_slow, a, b, kz, kk, pool)
-    gaps = jnp.concatenate([first_end, end, their_end]) - following
-    beyond = slow(jnp.concatenate([gaps, own[2:], theirs[3:]]))
-    late = fast(jnp.concatenate([gaps[:1], beyond[:4]]))
+        12,
+    )(at, near_slow, from_slow, a, b, kz, kk, pool, own, theirs, end, mate_end)
+    beyond = slow(first)
+    late = fast(jnp.concatenate([first[:1], beyond[:4]]))
 
     line = jnp.stack(
-        [beyond[2], beyond[1], beyond[0], gaps[0], gaps[1], gaps[2], late[0], late[1], late[2], late[3]]
+        [beyond[2], beyond[1], beyond[0], first[0], first[1], first[2], late[0], late[1], late[2], late[3]]
     )
     pairs = []
     for i in range(count):
@@ -421,11 +443,16 @@
     far = lax.ppermute(line, ("tm", "space"), [(i, (slices - 1) * count + i) for i in range(1, count, 2)])
     cc = jnp.stack([beyond[5], beyond[4], beyond[3], own[2], own[3], theirs[3], theirs[2], late[4]])
     ckz, ck = call(weights_kernel, [(7,) + block, (6, 5) + block], [], 100_000, 2)(at, cc)
+    own_start = jnp.concatenate([before, own[:2], theirs[1:2]])
     other = fast(jnp.concatenate([near, far]))
-    (result,) = call(final_kernel, [(planes,) + plane], [], 1_000_000, 10)(
-        at, near, far, other, ckz, ck, spread, tall, lower, upper
-    )
-    return result
+    return pl.pallas_call(
+        final_kernel,
+        out_shape=jax.ShapeDtypeStruct((planes,) + plane, F32),
+        in_specs=[pl.BlockSpec(memory_space=pltpu.SMEM)] + [pl.BlockSpec(memory_space=pltpu.VMEM)] * 10,
+        out_specs=pl.BlockSpec(memory_space=pl.ANY),
+        scratch_shapes=[pltpu.VMEM((2, HALF) + plane, F32), pltpu.SemaphoreType.DMA((2,))],
+        compiler_params=pltpu.CompilerParams(vmem_limit_bytes=VMEM_LIMIT),
+    )(at, near, far, other, own_start, ckz, ck, spread, tall, lower, upper)
 
 
 def solution(mesh):

time: 45.7 us -> 43.9 us (0.961)
  the two profiles are of different devices: /device:TPU:161 before, /device:TPU:31 now
where the time goes in v3:
time: 43.9 us; the launch traced here: 43.7 us
  starting transfers between devices  17.4 us (40%)
  waiting for transfers between devices  15.8 us (36%)
  Pallas kernels  10.2 us (23%)
    ppermute x2, waiting for transfers between devices, iteration(): slow = lambda x: lax.ppermute(x, 'space', slow_pairs)  13.4 us
    ppermute x2, starting transfers between devices, iteration(): slow = lambda x: lax.ppermute(x, 'space', slow_pairs)  6.05 us
    ppermute x1, starting transfers between devices, iteration(): near = lax.ppermute(line[1:9], ('tm', 'space'), pairs)  4.89 us
    ppermute x1, starting transfers between devices, iteration(): lax.ppermute(line, ('tm', 'space'), [(i, (slices - 1) * count + i) for i...  4.32 us
    pallas_call x1, Pallas kernels, iteration(): call(early_kernel, [(12,) + padded, (12,) + padded, (11,) + wide, (11, 5)...  3.13 us
    ppermute x5, starting transfers between devices, iteration(): fast = lambda x: lax.ppermute(x, 'space', fast_pairs)  2.13 us
    pallas_call x1, Pallas kernels, iteration(): call(late_kernel, [(4,) + wide, (6,) + block, (1,) + block], [(10,) + pad...  1.95 us
    pallas_call x1, Pallas kernels, iteration(): pl.pallas_call(final_kernel, out_shape=jax.ShapeDtypeStruct((planes,) + p...  1.91 us
  transfers between devices with their start and end apart: 9, of which 5 were waited for; matrix products, arithmetic and copies ran while one was open for 0% of the time, Pallas kernels for 10%

profile of v3, /device:TPU:31, one launch (start us, length us, event | category | flops | bytes accessed | tf_op | source)
XLA Modules:
  0.0 43.7 jit_solution(212967178578489875)
XLA Ops:
  0.0 0.1 pad_add_fusion.at
  0.1 1.8 %shard_map.28 = (f32[8,64,256]{2,1,0:T(8,128)S(1)}, f32[8,64,256]{2,1,0:T(8,128)S(1)}, bf16[512,128]{1,0:T(8,128)(2,1)S(1)}, bf16[128,512]{1,0:T(8,128)(2,1)S(1)}, bf16[64,16]{1,0:T(8,128)(2,1)S(1)}) custom-call(s32[4]{0:T(128)S(1)} %pad_add_fusion.at, f32[8,64,256]{2,1,0:T(8,128)} %bitcast.6, f32[8,64,256]{2,1,0:T(8,128)} %c.1), custom_call_target="tpu_custom_call" | custom-call | tf_op jit(solution)/shard_map/pallas_call | solution.py:403
  1.9 0.8 %collective-permute-start.1 = (f32[8,64,256]{2,1,0:T(8,128)S(1)}, f32[8,64,256]{2,1,0:T(8,128)S(1)}, u32[]{:S(2)}, u32[]{:S(2)}) collective-permute-start(f32[8,64,256]{2,1,0:T(8,128)S(1)} %get-tuple-element.22.near_fast), channel_id=1, source_target_pairs={{0,1},{1,0},{2,3},{3,2},{4,5},{5,4},{6,7},{7,6},{8,9},{9,8},{10,11... | collective-permute-start | bytes 1572872 | tf_op jit(solution)/shard_map/ppermute | solution.py:400
  2.6 3.0 %collective-permute-start = (f32[8,64,256]{2,1,0:T(8,128)S(1)}, f32[8,64,256]{2,1,0:T(8,128)S(1)}, u32[]{:S(2)}, u32[]{:S(2)}) collective-permute-start(f32[8,64,256]{2,1,0:T(8,128)S(1)} %get-tuple-element.21.near_slow), channel_id=1, source_target_pairs={{1,2},{3,4},{5,6},{7,8},{9,10},{11,12},{13,14},{15,16},{17,18},{19... | collective-permute-start | bytes 1572872 | tf_op jit(solution)/shard_map/ppermute | solution.py:399
  5.6 0.8 %shard_map.30.own = f32[4,8,128]{2,1,0:T(8,128)S(1)} custom-call(s32[4]{0:T(128)S(1)} %pad_add_fusion.at, f32[8,64,256]{2,1,0:T(8,128)S(1)} %get-tuple-element.21.near_slow, f32[8,64,256]{2,1,0:T(8,128)S(1)} %get-tuple-element.22.near_fast, bf16[512,128]{1,0:T(8,128)(2,1)S(1)} %get-tuple-element.23.pool), custom_call_target="tpu_custom_call" | custom-call | flops 1000000 | bytes 250000 | tf_op jit(solution)/shard_map/pallas_call | solution.py:415
  6.5 0.1 collective-permute-start.2
  6.6 0.0 collective-permute-done.1.h
  6.6 3.1 %shard_map.29 = (f32[12,2,80,128]{3,2,1,0:T(8,128)S(1)}, f32[12,2,80,128]{3,2,1,0:T(8,128)S(1)}, f32[11,2,64,128]{3,2,1,0:T(8,128)S(1)}, f32[11,5,2,64,128]{4,3,...) custom-call(s32[4]{0:T(128)S(1)} %pad_add_fusion.at, ...), custom_call_target="tpu_custom_call" | custom-call | flops 8000000 | bytes 2000000 | tf_op jit(solution)/shard_map/pallas_call | solution.py:417
  9.7 0.6 %collective-permute-start.3 = (f32[1,8,128]{2,1,0:T(8,128)S(1)}, f32[1,8,128]{2,1,0:T(8,128)S(1)}, u32[]{:S(2)}, u32[]{:S(2)}) collective-permute-start(f32[1,8,128]{2,1,0:T(8,128)S(1)} %get-tuple-element.28.end), channel_id=1, source_target_pairs={{0,1},{1,0},{2,3},{3,2},{4,5},{5,4},{6,7},{7,6},{8,9},{9,8},{10,11... | collective-permute-start | bytes 12296 | tf_op jit(solution)/shard_map/ppermute | solution.py:400
  10.3 0.0 collective-permute-done.2.theirs
  10.3 7.0 %collective-permute-done.g = f32[8,64,256]{2,1,0:T(8,128)S(1)} collective-permute-done((f32[8,64,256]{2,1,0:T(8,128)S(1)}, f32[8,64,256]{2,1,0:T(8,128)S(1)}, u32[]{:S(2)}, u32[]{:S(2)}) %collective-permute-start) | collective-permute-done | bytes 524320 | tf_op jit(solution)/shard_map/ppermute | solution.py:399
  17.3 0.0 collective-permute-done.3.mate_end
  17.3 1.9 %shard_map.31 = (f32[4,2,64,128]{3,2,1,0:T(8,128)S(1)}, f32[6,8,128]{2,1,0:T(8,128)S(1)}, f32[1,8,128]{2,1,0:T(8,128)S(1)}) custom-call(s32[4]{0:T(128)S(1)} %pad_add_fusion.at, f32[8,64,256]{2,1,0:T(8,128)S(1)} %get-tuple-element.21.near_slow, f32[8,64,256]{2,1,0:T(8,128)S(1)} %collective-permute-done.g, f32[12,2,80,128]{3,2,1,0:T(8,128)S(1)} %get-tuple-element.24.a, ...), custom_call_target="tpu_custom_call" | custom-call | flops 4000000 | bytes 1000000 | tf_op jit(solution)/shard_map/pallas_call | solution.py:425
  19.3 3.0 %collective-permute-start.4 = (f32[6,8,128]{2,1,0:T(8,128)S(1)}, f32[6,8,128]{2,1,0:T(8,128)S(1)}, u32[]{:S(2)}, u32[]{:S(2)}) collective-permute-start(f32[6,8,128]{2,1,0:T(8,128)S(1)} %get-tuple-element.29), channel_id=1, source_target_pairs={{1,2},{3,4},{5,6},{7,8},{9,10},{11,12},{13,14},{15,16},{17,18},{19... | collective-permute-start | bytes 73736 | tf_op jit(solution)/shard_map/ppermute | solution.py:399
  22.3 6.3 %collective-permute-done.4 = f32[6,8,128]{2,1,0:T(8,128)S(1)} collective-permute-done((f32[6,8,128]{2,1,0:T(8,128)S(1)}, f32[6,8,128]{2,1,0:T(8,128)S(1)}, u32[]{:S(2)}, u32[]{:S(2)}) %collective-permute-start.4) | collective-permute-done | bytes 24608 | tf_op jit(solution)/shard_map/ppermute | solution.py:399
  28.7 0.1 collective-permute-start.5
  28.8 1.1 %collective-permute-done.5 = f32[5,8,128]{2,1,0:T(8,128)S(1)} collective-permute-done((f32[5,8,128]{2,1,0:T(8,128)S(1)}, f32[5,8,128]{2,1,0:T(8,128)S(1)}, u32[]{:S(2)}, u32[]{:S(2)}) %collective-permute-start.5) | collective-permute-done | bytes 20512 | tf_op jit(solution)/shard_map/ppermute | solution.py:400
  30.0 4.9 %collective-permute-start.6 = (f32[8,8,128]{2,1,0:T(8,128)S(1)}, f32[8,8,128]{2,1,0:T(8,128)S(1)}, u32[]{:S(2)}, u32[]{:S(2)}) collective-permute-start(f32[8,8,128]{2,1,0:T(8,128)S(1)} %pad_maximum_fusion.1), channel_id=1, source_target_pairs={{0,128},{64,192},{1,65},{65,129},{129,193},{2,130},{66,194},{3,67}... | collective-permute-start | bytes 98312 | tf_op jit(solution)/shard_map/ppermute | solution.py:442
  34.9 4.3 %collective-permute-start.7 = (f32[10,8,128]{2,1,0:T(8,128)S(1)}, f32[10,8,128]{2,1,0:T(8,128)S(1)}, u32[]{:S(2)}, u32[]{:S(2)}) collective-permute-start(f32[10,8,128]{2,1,0:T(8,128)S(1)} %get-tuple-element.45), channel_id=1, source_target_pairs={{1,193},{3,195},{5,197},{7,199},{9,201},{11,203},{13,205},{15,207}... | collective-permute-start | bytes 122888 | tf_op jit(solution)/shard_map/ppermute | solution.py:443
  39.2 0.0 collective-permute-done.6.near
  39.2 1.1 %collective-permute-done.7.far = f32[10,8,128]{2,1,0:T(8,128)S(1)} collective-permute-done((f32[10,8,128]{2,1,0:T(8,128)S(1)}, f32[10,8,128]{2,1,0:T(8,128)S(1)}, u32[]{:S(2)}, u32[]{:S(2)}) %collective-permute-start.7) | collective-permute-done | bytes 40992 | tf_op jit(solution)/shard_map/ppermute | solution.py:443
  40.3 0.6 %collective-permute-start.8 = (f32[18,8,128]{2,1,0:T(8,128)S(1)}, f32[18,8,128]{2,1,0:T(8,128)S(1)}, u32[]{:S(2)}, u32[]{:S(2)}) collective-permute-start(f32[18,8,128]{2,1,0:T(8,128)S(1)} %pad_maximum_fusion), channel_id=1, source_target_pairs={{0,1},{1,0},{2,3},{3,2},{4,5},{5,4},{6,7},{7,6},{8,9},{9,8},{10,11... | collective-permute-start | bytes 221192 | tf_op jit(solution)/shard_map/ppermute | solution.py:400
  40.9 0.6 %shard_map.32 = (f32[7,8,128]{2,1,0:T(8,128)S(1)}, f32[6,5,8,128]{3,2,1,0:T(8,128)S(1)}) custom-call(s32[4]{0:T(128)S(1)} %pad_add_fusion.at, f32[8,8,128]{2,1,0:T(8,128)S(1)} %constant_dynamic-update-slice_fusion.5.cc), custom_call_target="tpu_custom_call" | custom-call | flops 100000 | bytes 25000 | tf_op jit(solution)/shard_map/pallas_call | solution.py:445
  41.5 0.3 collective-permute-done.8.other
  41.8 1.9 %shard_map.33 = f32[8,64,256]{2,1,0:T(8,128)} custom-call(s32[4]{0:T(128)S(1)} %pad_add_fusion.at, f32[8,8,128]{2,1,0:T(8,128)S(1)} %collective-permute-done.6.near, f32[10,8,128]{2,1,0:T(8,128)S(1)} %collective-permute-done.7.far, f32[18,8,128]{2,1,0:T(8,128)S(1)} %collective-permute-done.8.other, f32[4,8,128]{2,1,0:T(8,128)S(1)} %pad_maximum_fusion.5.own_start, ...), custom_call_target="tpu_custom_call" | custom-call | tf_op jit(solution)/shard_map/pallas_call | solution.py:448
  (16 shorter events, 0.1 us)
Async XLA Ops:
  1.9 4.7 %collective-permute-start.1 = (f32[8,64,256]{2,1,0:T(8,128)S(1)}, f32[8,64,256]{2,1,0:T(8,128)S(1)}, u32[]{:S(2)}, u32[]{:S(2)}) collective-permute-start(f32[8,64,256]{2,1,0:T(8,128)S(1)} %get-tuple-element.22.near_fast), channel_id=1, source_target_pairs={{0,1},{1,0},{2,3},{3,2},{4,5},{5,4},{6,7},{7,6},{8,9},{9,8},{10,11... | collective-permute-start | bytes 1572872 | tf_op jit(solution)/shard_map/ppermute | solution.py:400
  2.6 14.7 %collective-permute-start = (f32[8,64,256]{2,1,0:T(8,128)S(1)}, f32[8,64,256]{2,1,0:T(8,128)S(1)}, u32[]{:S(2)}, u32[]{:S(2)}) collective-permute-start(f32[8,64,256]{2,1,0:T(8,128)S(1)} %get-tuple-element.21.near_slow), channel_id=1, source_target_pairs={{1,2},{3,4},{5,6},{7,8},{9,10},{11,12},{13,14},{15,16},{17,18},{19... | collective-permute-start | bytes 1572872 | tf_op jit(solution)/shard_map/ppermute | solution.py:399
  6.5 3.8 %collective-permute-start.2 = (f32[4,8,128]{2,1,0:T(8,128)S(1)}, f32[4,8,128]{2,1,0:T(8,128)S(1)}, u32[]{:S(2)}, u32[]{:S(2)}) collective-permute-start(f32[4,8,128]{2,1,0:T(8,128)S(1)} %shard_map.30.own), channel_id=1, source_target_pairs={{0,1},{1,0},{2,3},{3,2},{4,5},{5,4},{6,7},{7,6},{8,9},{9,8},{10,11... | collective-permute-start | bytes 49160 | tf_op jit(solution)/shard_map/ppermute | solution.py:400
  9.7 7.6 %collective-permute-start.3 = (f32[1,8,128]{2,1,0:T(8,128)S(1)}, f32[1,8,128]{2,1,0:T(8,128)S(1)}, u32[]{:S(2)}, u32[]{:S(2)}) collective-permute-start(f32[1,8,128]{2,1,0:T(8,128)S(1)} %get-tuple-element.28.end), channel_id=1, source_target_pairs={{0,1},{1,0},{2,3},{3,2},{4,5},{5,4},{6,7},{7,6},{8,9},{9,8},{10,11... | collective-permute-start | bytes 12296 | tf_op jit(solution)/shard_map/ppermute | solution.py:400
  19.3 9.4 %collective-permute-start.4 = (f32[6,8,128]{2,1,0:T(8,128)S(1)}, f32[6,8,128]{2,1,0:T(8,128)S(1)}, u32[]{:S(2)}, u32[]{:S(2)}) collective-permute-start(f32[6,8,128]{2,1,0:T(8,128)S(1)} %get-tuple-element.29), channel_id=1, source_target_pairs={{1,2},{3,4},{5,6},{7,8},{9,10},{11,12},{13,14},{15,16},{17,18},{19... | collective-permute-start | bytes 73736 | tf_op jit(solution)/shard_map/ppermute | solution.py:399
  28.7 1.3 %collective-permute-start.5 = (f32[5,8,128]{2,1,0:T(8,128)S(1)}, f32[5,8,128]{2,1,0:T(8,128)S(1)}, u32[]{:S(2)}, u32[]{:S(2)}) collective-permute-start(f32[5,8,128]{2,1,0:T(8,128)S(1)} %pad_maximum_fusion.4), channel_id=1, source_target_pairs={{0,1},{1,0},{2,3},{3,2},{4,5},{5,4},{6,7},{7,6},{8,9},{9,8},{10,11... | collective-permute-start | bytes 61448 | tf_op jit(solution)/shard_map/ppermute | solution.py:400
  30.0 9.2 %collective-permute-start.6 = (f32[8,8,128]{2,1,0:T(8,128)S(1)}, f32[8,8,128]{2,1,0:T(8,128)S(1)}, u32[]{:S(2)}, u32[]{:S(2)}) collective-permute-start(f32[8,8,128]{2,1,0:T(8,128)S(1)} %pad_maximum_fusion.1), channel_id=1, source_target_pairs={{0,128},{64,192},{1,65},{65,129},{129,193},{2,130},{66,194},{3,67}... | collective-permute-start | bytes 98312 | tf_op jit(solution)/shard_map/ppermute | solution.py:442
  34.9 5.4 %collective-permute-start.7 = (f32[10,8,128]{2,1,0:T(8,128)S(1)}, f32[10,8,128]{2,1,0:T(8,128)S(1)}, u32[]{:S(2)}, u32[]{:S(2)}) collective-permute-start(f32[10,8,128]{2,1,0:T(8,128)S(1)} %get-tuple-element.45), channel_id=1, source_target_pairs={{1,193},{3,195},{5,197},{7,199},{9,201},{11,203},{13,205},{15,207}... | collective-permute-start | bytes 122888 | tf_op jit(solution)/shard_map/ppermute | solution.py:443
  40.3 1.5 %collective-permute-start.8 = (f32[18,8,128]{2,1,0:T(8,128)S(1)}, f32[18,8,128]{2,1,0:T(8,128)S(1)}, u32[]{:S(2)}, u32[]{:S(2)}) collective-permute-start(f32[18,8,128]{2,1,0:T(8,128)S(1)} %pad_maximum_fusion), channel_id=1, source_target_pairs={{0,1},{1,0},{2,3},{3,2},{4,5},{5,4},{6,7},{7,6},{8,9},{9,8},{10,11... | collective-permute-start | bytes 221192 | tf_op jit(solution)/shard_map/ppermute | solution.py:400

commit v4 on v3

--- a/solution.py
+++ b/solution.py
@@ -20,6 +20,13 @@
 PADDED = 80
 UNROLL = True
 CHUNK = 8
+
+
+def place():
+    k, count = lax.axis_index("space"), lax.axis_size("space")
+    inside = lambda i: (i != 0) & (i != count - 1)
+    par = k % 2
+    return par, inside(k), inside(k + 1 - 2 * par), lax.axis_index("tm")
 
 
 def fast_plane(par, i):
@@ -161,8 +168,8 @@
     return jnp.where(same, 1.0, 0.0).astype(BF16)
 
 
-def pack_kernel(at, v, c, near_slow, near_fast, pool, spread, tall, sems):
-    par = at[0]
+def pack_kernel(v, c, near_slow, near_fast, pool, spread, tall, sems):
+    par = place()[0]
     copies = []
     for s, (ref, side) in enumerate(((near_slow, par), (near_fast, 1 - par))):
         for f, src in enumerate((v, c)):
@@ -188,16 +195,16 @@
             put(coefficient, base + i, ref[HALF + fast_plane(par, i)])
 
 
-def coarse_kernel(at, near_slow, near_fast, pool, out, v0, c0):
-    put_own(at[0], near_slow, near_fast, v0, c0)
+def coarse_kernel(near_slow, near_fast, pool, out, v0, c0):
+    put_own(place()[0], near_slow, near_fast, v0, c0)
     sums = [block_sums(ref, 4 * b, TOP) for ref in (v0, c0) for b in range(2)]
     res = pooled(jnp.concatenate(sums, axis=0), pool[...])
     for i in range(4):
         out[i] = res[8 * i : 8 * i + 8]
 
 
-def early_kernel(at, near_slow, near_fast, h, pool, a, b, kz, k, fine, end, c0):
-    par = at[0]
+def early_kernel(near_slow, near_fast, h, pool, a, b, kz, k, fine, end, c0):
+    par = place()[0]
     blank_margins(a, 12)
     blank_margins(b, 12)
     put_own(par, near_slow, near_fast, a, c0)
@@ -255,9 +262,9 @@
 
 
 def late_kernel(
-    at, near_slow, g, a, b, kz, k, pool, own, theirs, end, mate_end, fine, out, before, v0, c0, w0, kl, kzl
+    near_slow, g, a, b, kz, k, pool, own, theirs, end, mate_end, fine, out, before, v0, c0, w0, kl, kzl
 ):
-    par = at[0]
+    par = place()[0]
     blank_margins(v0, 10)
     blank_margins(w0, 10)
 
@@ -275,21 +282,21 @@
     start = [beyond[:8], own[0], own[1], theirs[1], theirs[0]]
     cc = [beyond[8:], own[2], own[3], theirs[3], theirs[2]]
     faces = [(cc[i] + cc[i + 1]) * (0.5 * COARSE_RATE) for i in range(4)]
-    faces[0] = jnp.where(at[1] > 0, faces[0], 0.0)
+    faces[0] = jnp.where(place()[1], faces[0], 0.0)
     masks = coarse_masks()
     before[0] = start[0]
     stepped = []
     for i in range(1, 4):
         w = coarse_weights(cc[i], faces[i] + faces[i - 1], masks)
         step = coarse_step(start[i], start[i + 1], start[i - 1], faces[i], faces[i - 1], w)
-        stepped.append(jnp.where(at[3] > 0, step, 0.0))
+        stepped.append(jnp.where(place()[3] > 0, step, 0.0))
         out[2 + i] = cc[i]
     out[1] = end[0] - stepped[1]
     out[2] = mate_end[0] - stepped[2]
     scale = 0.5 * FINE_RATE
     fill_faces(c0, kzl, 0, 5, scale, True)
     for h in range(2):
-        kzl[3, h] = jnp.where(at[1] > 0, kzl[3, h], 0.0)
+        kzl[3, h] = jnp.where(place()[1], kzl[3, h], 0.0)
     fill_coefficients(c0, kzl, kl, 1, 5, scale, True)
     advance(v0, into(w0), kzl, kl, 1, 5, True)
     for h in range(2):
@@ -310,11 +317,11 @@
     out[0] = pooled(block_sums(fine, 0, 0), pool[...]) - stepped[0]
 
 
-def weights_kernel(at, cc, kz, k):
+def weights_kernel(cc, kz, k):
     masks = coarse_masks()
     faces = [(cc[i] + cc[i + 1]) * (0.5 * COARSE_RATE) for i in range(7)]
-    faces[2] = jnp.where(at[1] > 0, faces[2], 0.0)
-    faces[6] = jnp.where(at[2] > 0, faces[6], 0.0)
+    faces[2] = jnp.where(place()[1], faces[2], 0.0)
+    faces[6] = jnp.where(place()[2], faces[6], 0.0)
     for i in range(7):
         kz[i] = faces[i]
     for i in range(6):
@@ -322,8 +329,8 @@
             k[i, f] = a
 
 
-def final_kernel(at, near, far, other, own_start, kz, k, spread, tall, lower, upper, out, made, sems):
-    par, slice_at = at[0], at[3]
+def final_kernel(near, far, other, own_start, kz, k, spread, tall, lower, upper, out, made, sems):
+    par, _, _, slice_at = place()
 
     def pick(level, p):
         return jnp.where((par == 1) == (level == 1), near[p + 2], other[5 - p])
@@ -369,8 +376,7 @@
     return pl.pallas_call(
         kernel,
         out_shape=[jax.ShapeDtypeStruct(s, F32) for s in outs],
-        in_specs=[pl.BlockSpec(memory_space=pltpu.SMEM)]
-        + [pl.BlockSpec(memory_space=pltpu.VMEM)] * (count - 1),
+        in_specs=[pl.BlockSpec(memory_space=pltpu.VMEM)] * count,
         out_specs=[pl.BlockSpec(memory_space=pltpu.VMEM)] * len(outs),
         scratch_shapes=[pltpu.VMEM(s, F32) for s in scratch],
         compiler_params=pltpu.CompilerParams(vmem_limit_bytes=VMEM_LIMIT),
@@ -386,12 +392,7 @@
     planes, rows, cols = v.shape
     plane = (rows, cols)
     wide, padded, block = (2, ROWS, LANES), (2, PADDED, LANES), (8, LANES)
-    k, n = lax.axis_index("space"), lax.axis_index("tm")
     count, slices = lax.axis_size("space"), lax.axis_size("tm")
-    par = k % 2
-    mate = k + 1 - 2 * par
-    inside = lambda i: ((i != 0) & (i != count - 1)).astype(jnp.int32)
-    at = jnp.stack([par, inside(k), inside(mate), n]).astype(jnp.int32)
 
     slow_pairs = [(i, i + 1) for i in range(1, count - 1, 2)]
     slow_pairs += [(b, a) for a, b in slow_pairs]
@@ -404,31 +405,31 @@
         pack_kernel,
         out_shape=[jax.ShapeDtypeStruct(half, F32)] * 2
         + [jax.ShapeDtypeStruct(m, BF16) for m in ((512, LANES), (LANES, 512), (64, 16))],
-        in_specs=[pl.BlockSpec(memory_space=pltpu.SMEM)] + [pl.BlockSpec(memory_space=pltpu.HBM)] * 2,
+        in_specs=[pl.BlockSpec(memory_space=pltpu.HBM)] * 2,
         out_specs=[pl.BlockSpec(memory_space=pltpu.VMEM)] * 5,
         scratch_shapes=[pltpu.SemaphoreType.DMA((4,))],
         compiler_params=pltpu.CompilerParams(vmem_limit_bytes=VMEM_LIMIT),
-    )(at, *(pltpu.with_memory_space_constraint(x, pltpu.HBM) for x in (v, c)))
+    )(*(pltpu.with_memory_space_constraint(x, pltpu.HBM) for x in (v, c)))
     from_slow = slow(near_slow)
     from_fast = fast(near_fast)
 
-    (own,) = call(coarse_kernel, [(4,) + block], [(8,) + padded] * 2, 1_000_000, 4)(at, near_slow, near_fast, pool)
+    (own,) = call(coarse_kernel, [(4,) + block], [(8,) + padded] * 2, 1_000_000, 3)(near_slow, near_fast, pool)
     theirs = fast(own)
     a, b, kz, kk, upper, end = call(
         early_kernel,
         [(12,) + padded, (12,) + padded, (11,) + wide, (11, 5) + wide, (4,) + wide, (1,) + block],
         [(12,) + padded],
         8_000_000,
-        5,
-    )(at, near_slow, near_fast, from_fast, pool)
+        4,
+    )(near_slow, near_fast, from_fast, pool)
     mate_end = fast(end)
     lower, first, before = call(
         late_kernel,
         [(4,) + wide, (6,) + block, (1,) + block],
         [(10,) + padded] * 3 + [(5, 5) + wide, (5,) + wide],
         4_000_000,
-        12,
-    )(at, near_slow, from_slow, a, b, kz, kk, pool, own, theirs, end, mate_end)
+        11,
+    )(near_slow, from_slow, a, b, kz, kk, pool, own, theirs, end, mate_end)
     beyond = slow(first)
     late = fast(jnp.concatenate([first[:1], beyond[:4]]))
 
@@ -442,17 +443,17 @@
     near = lax.ppermute(line[1:9], ("tm", "space"), pairs)
     far = lax.ppermute(line, ("tm", "space"), [(i, (slices - 1) * count + i) for i in range(1, count, 2)])
     cc = jnp.stack([beyond[5], beyond[4], beyond[3], own[2], own[3], theirs[3], theirs[2], late[4]])
-    ckz, ck = call(weights_kernel, [(7,) + block, (6, 5) + block], [], 100_000, 2)(at, cc)
+    ckz, ck = call(weights_kernel, [(7,) + block, (6, 5) + block], [], 100_000, 1)(cc)
     own_start = jnp.concatenate([before, own[:2], theirs[1:2]])
     other = fast(jnp.concatenate([near, far]))
     return pl.pallas_call(
         final_kernel,
         out_shape=jax.ShapeDtypeStruct((planes,) + plane, F32),
-        in_specs=[pl.BlockSpec(memory_space=pltpu.SMEM)] + [pl.BlockSpec(memory_space=pltpu.VMEM)] * 10,
+        in_specs=[pl.BlockSpec(memory_space=pltpu.VMEM)] * 10,
         out_specs=pl.BlockSpec(memory_space=pl.ANY),
         scratch_shapes=[pltpu.VMEM((2, HALF) + plane, F32), pltpu.SemaphoreType.DMA((2,))],
         compiler_params=pltpu.CompilerParams(vmem_limit_bytes=VMEM_LIMIT),
-    )(at, near, far, other, own_start, ckz, ck, spread, tall, lower, upper)
+    )(near, far, other, own_start, ckz, ck, spread, tall, lower, upper)
 
 
 def solution(mesh):

time: 43.9 us -> 42.1 us (0.959)
  Pallas kernels: 10.2 us -> 6.84 us
  waiting for transfers between devices: 15.8 us -> 17.5 us
    ppermute x2, waiting for transfers between devices: 13.4 us -> 14.5 us  [iteration(): slow = lambda x: lax.ppermute(x, 'space', slow_pairs)]
    pallas_call x2, Pallas kernels: 1.44 us -> 0.37 us  [the longest x1 0.28 us: iteration(): call(coarse_kernel, [(4,) + block], [(8,) + padded] * 2, 1000000, 3)]
    pallas_call x1, Pallas kernels: 1.95 us -> 1.33 us  [iteration(): call(late_kernel, [(4,) + wide, (6,) + block, (1,) + block], [(10,) + pad...]
    pallas_call x1, Pallas kernels: 3.13 us -> 2.54 us  [iteration(): call(early_kernel, [(12,) + padded, (12,) + padded, (11,) + wide, (11, 5)...]
    pallas_call x1, Pallas kernels: 1.91 us -> 1.37 us  [iteration(): pl.pallas_call(final_kernel, out_shape=jax.ShapeDtypeStruct((planes,) + p...]
    ppermute x5, waiting for transfers between devices: 1.42 us -> 1.95 us  [iteration(): fast = lambda x: lax.ppermute(x, 'space', fast_pairs)]
    pallas_call x1, Pallas kernels: 1.77 us -> 1.23 us  [iteration(): pl.pallas_call(pack_kernel, out_shape=[jax.ShapeDtypeStruct(half, F32)] *...]
  transfers between devices with their start and end apart: 9 -> 9, of which waited for: 5 -> 5; matrix products, arithmetic and copies ran while one was open for 0% -> 0% of each run, Pallas kernels for 10% -> 7%
where the time goes in v4:
time: 42.1 us; the launch traced here: 42 us
  waiting for transfers between devices  17.5 us (42%)
  starting transfers between devices  17.4 us (41%)
  Pallas kernels  6.84 us (16%)
    ppermute x2, waiting for transfers between devices, iteration(): slow = lambda x: lax.ppermute(x, 'space', slow_pairs)  14.5 us
    ppermute x2, starting transfers between devices, iteration(): slow = lambda x: lax.ppermute(x, 'space', slow_pairs)  6.05 us
    ppermute x1, starting transfers between devices, iteration(): near = lax.ppermute(line[1:9], ('tm', 'space'), pairs)  4.89 us
    ppermute x1, starting transfers between devices, iteration(): lax.ppermute(line, ('tm', 'space'), [(i, (slices - 1) * count + i) for i...  4.32 us
    pallas_call x1, Pallas kernels, iteration(): call(early_kernel, [(12,) + padded, (12,) + padded, (11,) + wide, (11, 5)...  2.54 us
    ppermute x5, starting transfers between devices, iteration(): fast = lambda x: lax.ppermute(x, 'space', fast_pairs)  2.12 us
    ppermute x5, waiting for transfers between devices, iteration(): fast = lambda x: lax.ppermute(x, 'space', fast_pairs)  1.95 us
    pallas_call x1, Pallas kernels, iteration(): pl.pallas_call(final_kernel, out_shape=jax.ShapeDtypeStruct((planes,) + p...  1.37 us
  transfers between devices with their start and end apart: 9, of which 5 were waited for; matrix products, arithmetic and copies ran while one was open for 0% of the time, Pallas kernels for 7%

profile of v4, /device:TPU:31, one launch (start us, length us, event | category | flops | bytes accessed | tf_op | source)
XLA Modules:
  0.0 42.0 jit_solution(14920150723298794331)
XLA Ops:
  0.0 1.2 %shard_map.28 = (f32[8,64,256]{2,1,0:T(8,128)S(1)}, f32[8,64,256]{2,1,0:T(8,128)S(1)}, bf16[512,128]{1,0:T(8,128)(2,1)S(1)}, bf16[128,512]{1,0:T(8,128)(2,1)S(1)}, bf16[64,16]{1,0:T(8,128)(2,1)S(1)}) custom-call(f32[8,64,256]{2,1,0:T(8,128)} %bitcast.2, f32[8,64,256]{2,1,0:T(8,128)} %c.1), custom_call_target="tpu_custom_call" | custom-call | tf_op jit(solution)/shard_map/pallas_call | solution.py:404
  1.2 0.8 %collective-permute-start.1 = (f32[8,64,256]{2,1,0:T(8,128)S(1)}, f32[8,64,256]{2,1,0:T(8,128)S(1)}, u32[]{:S(2)}, u32[]{:S(2)}) collective-permute-start(f32[8,64,256]{2,1,0:T(8,128)S(1)} %get-tuple-element.22.near_fast), channel_id=1, source_target_pairs={{0,1},{1,0},{2,3},{3,2},{4,5},{5,4},{6,7},{7,6},{8,9},{9,8},{10,11... | collective-permute-start | bytes 1572872 | tf_op jit(solution)/shard_map/ppermute | solution.py:401
  2.0 3.0 %collective-permute-start = (f32[8,64,256]{2,1,0:T(8,128)S(1)}, f32[8,64,256]{2,1,0:T(8,128)S(1)}, u32[]{:S(2)}, u32[]{:S(2)}) collective-permute-start(f32[8,64,256]{2,1,0:T(8,128)S(1)} %get-tuple-element.21.near_slow), channel_id=1, source_target_pairs={{1,2},{3,4},{5,6},{7,8},{9,10},{11,12},{13,14},{15,16},{17,18},{19... | collective-permute-start | bytes 1572872 | tf_op jit(solution)/shard_map/ppermute | solution.py:400
  5.0 0.3 shard_map.30.own
  5.3 0.1 collective-permute-start.2
  5.4 0.0 collective-permute-done.1.h
  5.4 2.5 %shard_map.29 = (f32[12,2,80,128]{3,2,1,0:T(8,128)S(1)}, f32[12,2,80,128]{3,2,1,0:T(8,128)S(1)}, f32[11,2,64,128]{3,2,1,0:T(8,128)S(1)}, f32[11,5,2,64,128]{4,3,...) custom-call(f32[8,64,256]{2,1,0:T(8,128)S(1)} %get-tuple-element.21.near_slow, ...), custom_call_target="tpu_custom_call" | custom-call | flops 8000000 | bytes 2000000 | tf_op jit(solution)/shard_map/pallas_call | solution.py:418
  8.0 0.6 %collective-permute-start.3 = (f32[1,8,128]{2,1,0:T(8,128)S(1)}, f32[1,8,128]{2,1,0:T(8,128)S(1)}, u32[]{:S(2)}, u32[]{:S(2)}) collective-permute-start(f32[1,8,128]{2,1,0:T(8,128)S(1)} %get-tuple-element.28.end), channel_id=1, source_target_pairs={{0,1},{1,0},{2,3},{3,2},{4,5},{5,4},{6,7},{7,6},{8,9},{9,8},{10,11... | collective-permute-start | bytes 12296 | tf_op jit(solution)/shard_map/ppermute | solution.py:401
  8.5 0.0 collective-permute-done.2.theirs
  8.5 8.2 %collective-permute-done.g = f32[8,64,256]{2,1,0:T(8,128)S(1)} collective-permute-done((f32[8,64,256]{2,1,0:T(8,128)S(1)}, f32[8,64,256]{2,1,0:T(8,128)S(1)}, u32[]{:S(2)}, u32[]{:S(2)}) %collective-permute-start) | collective-permute-done | bytes 524320 | tf_op jit(solution)/shard_map/ppermute | solution.py:400
  16.7 0.0 collective-permute-done.3.mate_end
  16.7 1.3 %shard_map.31 = (f32[4,2,64,128]{3,2,1,0:T(8,128)S(1)}, f32[6,8,128]{2,1,0:T(8,128)S(1)}, f32[1,8,128]{2,1,0:T(8,128)S(1)}) custom-call(f32[8,64,256]{2,1,0:T(8,128)S(1)} %get-tuple-element.21.near_slow, f32[8,64,256]{2,1,0:T(8,128)S(1)} %collective-permute-done.g, f32[12,2,80,128]{3,2,1,0:T(8,128)S(1)} %get-tuple-element.24.a, ...), custom_call_target="tpu_custom_call" | custom-call | flops 4000000 | bytes 1000000 | tf_op jit(solution)/shard_map/pallas_call | solution.py:426
  18.0 3.0 %collective-permute-start.4 = (f32[6,8,128]{2,1,0:T(8,128)S(1)}, f32[6,8,128]{2,1,0:T(8,128)S(1)}, u32[]{:S(2)}, u32[]{:S(2)}) collective-permute-start(f32[6,8,128]{2,1,0:T(8,128)S(1)} %get-tuple-element.29), channel_id=1, source_target_pairs={{1,2},{3,4},{5,6},{7,8},{9,10},{11,12},{13,14},{15,16},{17,18},{19... | collective-permute-start | bytes 73736 | tf_op jit(solution)/shard_map/ppermute | solution.py:400
  21.1 6.3 %collective-permute-done.4 = f32[6,8,128]{2,1,0:T(8,128)S(1)} collective-permute-done((f32[6,8,128]{2,1,0:T(8,128)S(1)}, f32[6,8,128]{2,1,0:T(8,128)S(1)}, u32[]{:S(2)}, u32[]{:S(2)}) %collective-permute-start.4) | collective-permute-done | bytes 24608 | tf_op jit(solution)/shard_map/ppermute | solution.py:400
  27.4 0.1 collective-permute-start.5
  27.6 1.1 %collective-permute-done.5 = f32[5,8,128]{2,1,0:T(8,128)S(1)} collective-permute-done((f32[5,8,128]{2,1,0:T(8,128)S(1)}, f32[5,8,128]{2,1,0:T(8,128)S(1)}, u32[]{:S(2)}, u32[]{:S(2)}) %collective-permute-start.5) | collective-permute-done | bytes 20512 | tf_op jit(solution)/shard_map/ppermute | solution.py:401
  28.7 4.9 %collective-permute-start.6 = (f32[8,8,128]{2,1,0:T(8,128)S(1)}, f32[8,8,128]{2,1,0:T(8,128)S(1)}, u32[]{:S(2)}, u32[]{:S(2)}) collective-permute-start(f32[8,8,128]{2,1,0:T(8,128)S(1)} %pad_maximum_fusion.1), channel_id=1, source_target_pairs={{0,128},{64,192},{1,65},{65,129},{129,193},{2,130},{66,194},{3,67}... | collective-permute-start | bytes 98312 | tf_op jit(solution)/shard_map/ppermute | solution.py:443
  33.6 4.3 %collective-permute-start.7 = (f32[10,8,128]{2,1,0:T(8,128)S(1)}, f32[10,8,128]{2,1,0:T(8,128)S(1)}, u32[]{:S(2)}, u32[]{:S(2)}) collective-permute-start(f32[10,8,128]{2,1,0:T(8,128)S(1)} %get-tuple-element.45), channel_id=1, source_target_pairs={{1,193},{3,195},{5,197},{7,199},{9,201},{11,203},{13,205},{15,207}... | collective-permute-start | bytes 122888 | tf_op jit(solution)/shard_map/ppermute | solution.py:444
  38.0 0.0 collective-permute-done.6.near
  38.0 1.1 %collective-permute-done.7.far = f32[10,8,128]{2,1,0:T(8,128)S(1)} collective-permute-done((f32[10,8,128]{2,1,0:T(8,128)S(1)}, f32[10,8,128]{2,1,0:T(8,128)S(1)}, u32[]{:S(2)}, u32[]{:S(2)}) %collective-permute-start.7) | collective-permute-done | bytes 40992 | tf_op jit(solution)/shard_map/ppermute | solution.py:444
  39.1 0.6 %collective-permute-start.8 = (f32[18,8,128]{2,1,0:T(8,128)S(1)}, f32[18,8,128]{2,1,0:T(8,128)S(1)}, u32[]{:S(2)}, u32[]{:S(2)}) collective-permute-start(f32[18,8,128]{2,1,0:T(8,128)S(1)} %pad_maximum_fusion), channel_id=1, source_target_pairs={{0,1},{1,0},{2,3},{3,2},{4,5},{5,4},{6,7},{7,6},{8,9},{9,8},{10,11... | collective-permute-start | bytes 221192 | tf_op jit(solution)/shard_map/ppermute | solution.py:401
  39.7 0.1 shard_map.32
  39.8 0.8 %collective-permute-done.8.other = f32[18,8,128]{2,1,0:T(8,128)S(1)} collective-permute-done((f32[18,8,128]{2,1,0:T(8,128)S(1)}, f32[18,8,128]{2,1,0:T(8,128)S(1)}, u32[]{:S(2)}, u32[]{:S(2)}) %collective-permute-start.8) | collective-permute-done | bytes 73760 | tf_op jit(solution)/shard_map/ppermute | solution.py:401
  40.6 1.4 %shard_map.33 = f32[8,64,256]{2,1,0:T(8,128)} custom-call(f32[8,8,128]{2,1,0:T(8,128)S(1)} %collective-permute-done.6.near, f32[10,8,128]{2,1,0:T(8,128)S(1)} %collective-permute-done.7.far, f32[18,8,128]{2,1,0:T(8,128)S(1)} %collective-permute-done.8.other, f32[4,8,128]{2,1,0:T(8,128)S(1)} %pad_maximum_fusion.5.own_start, ...), custom_call_target="tpu_custom_call" | custom-call | tf_op jit(solution)/shard_map/pallas_call | solution.py:449
  (16 shorter events, 0.1 us)
Async XLA Ops:
  1.2 4.2 %collective-permute-start.1 = (f32[8,64,256]{2,1,0:T(8,128)S(1)}, f32[8,64,256]{2,1,0:T(8,128)S(1)}, u32[]{:S(2)}, u32[]{:S(2)}) collective-permute-start(f32[8,64,256]{2,1,0:T(8,128)S(1)} %get-tuple-element.22.near_fast), channel_id=1, source_target_pairs={{0,1},{1,0},{2,3},{3,2},{4,5},{5,4},{6,7},{7,6},{8,9},{9,8},{10,11... | collective-permute-start | bytes 1572872 | tf_op jit(solution)/shard_map/ppermute | solution.py:401
  2.0 14.7 %collective-permute-start = (f32[8,64,256]{2,1,0:T(8,128)S(1)}, f32[8,64,256]{2,1,0:T(8,128)S(1)}, u32[]{:S(2)}, u32[]{:S(2)}) collective-permute-start(f32[8,64,256]{2,1,0:T(8,128)S(1)} %get-tuple-element.21.near_slow), channel_id=1, source_target_pairs={{1,2},{3,4},{5,6},{7,8},{9,10},{11,12},{13,14},{15,16},{17,18},{19... | collective-permute-start | bytes 1572872 | tf_op jit(solution)/shard_map/ppermute | solution.py:400
  5.3 3.2 %collective-permute-start.2 = (f32[4,8,128]{2,1,0:T(8,128)S(1)}, f32[4,8,128]{2,1,0:T(8,128)S(1)}, u32[]{:S(2)}, u32[]{:S(2)}) collective-permute-start(f32[4,8,128]{2,1,0:T(8,128)S(1)} %shard_map.30.own), channel_id=1, source_target_pairs={{0,1},{1,0},{2,3},{3,2},{4,5},{5,4},{6,7},{7,6},{8,9},{9,8},{10,11... | collective-permute-start | bytes 49160 | tf_op jit(solution)/shard_map/ppermute | solution.py:401
  8.0 8.7 %collective-permute-start.3 = (f32[1,8,128]{2,1,0:T(8,128)S(1)}, f32[1,8,128]{2,1,0:T(8,128)S(1)}, u32[]{:S(2)}, u32[]{:S(2)}) collective-permute-start(f32[1,8,128]{2,1,0:T(8,128)S(1)} %get-tuple-element.28.end), channel_id=1, source_target_pairs={{0,1},{1,0},{2,3},{3,2},{4,5},{5,4},{6,7},{7,6},{8,9},{9,8},{10,11... | collective-permute-start | bytes 12296 | tf_op jit(solution)/shard_map/ppermute | solution.py:401
  18.0 9.4 %collective-permute-start.4 = (f32[6,8,128]{2,1,0:T(8,128)S(1)}, f32[6,8,128]{2,1,0:T(8,128)S(1)}, u32[]{:S(2)}, u32[]{:S(2)}) collective-permute-start(f32[6,8,128]{2,1,0:T(8,128)S(1)} %get-tuple-element.29), channel_id=1, source_target_pairs={{1,2},{3,4},{5,6},{7,8},{9,10},{11,12},{13,14},{15,16},{17,18},{19... | collective-permute-start | bytes 73736 | tf_op jit(solution)/shard_map/ppermute | solution.py:400
  27.4 1.3 %collective-permute-start.5 = (f32[5,8,128]{2,1,0:T(8,128)S(1)}, f32[5,8,128]{2,1,0:T(8,128)S(1)}, u32[]{:S(2)}, u32[]{:S(2)}) collective-permute-start(f32[5,8,128]{2,1,0:T(8,128)S(1)} %pad_maximum_fusion.4), channel_id=1, source_target_pairs={{0,1},{1,0},{2,3},{3,2},{4,5},{5,4},{6,7},{7,6},{8,9},{9,8},{10,11... | collective-permute-start | bytes 61448 | tf_op jit(solution)/shard_map/ppermute | solution.py:401
  28.7 9.2 %collective-permute-start.6 = (f32[8,8,128]{2,1,0:T(8,128)S(1)}, f32[8,8,128]{2,1,0:T(8,128)S(1)}, u32[]{:S(2)}, u32[]{:S(2)}) collective-permute-start(f32[8,8,128]{2,1,0:T(8,128)S(1)} %pad_maximum_fusion.1), channel_id=1, source_target_pairs={{0,128},{64,192},{1,65},{65,129},{129,193},{2,130},{66,194},{3,67}... | collective-permute-start | bytes 98312 | tf_op jit(solution)/shard_map/ppermute | solution.py:443
  33.6 5.4 %collective-permute-start.7 = (f32[10,8,128]{2,1,0:T(8,128)S(1)}, f32[10,8,128]{2,1,0:T(8,128)S(1)}, u32[]{:S(2)}, u32[]{:S(2)}) collective-permute-start(f32[10,8,128]{2,1,0:T(8,128)S(1)} %get-tuple-element.45), channel_id=1, source_target_pairs={{1,193},{3,195},{5,197},{7,199},{9,201},{11,203},{13,205},{15,207}... | collective-permute-start | bytes 122888 | tf_op jit(solution)/shard_map/ppermute | solution.py:444
  39.1 1.5 %collective-permute-start.8 = (f32[18,8,128]{2,1,0:T(8,128)S(1)}, f32[18,8,128]{2,1,0:T(8,128)S(1)}, u32[]{:S(2)}, u32[]{:S(2)}) collective-permute-start(f32[18,8,128]{2,1,0:T(8,128)S(1)} %pad_maximum_fusion), channel_id=1, source_target_pairs={{0,1},{1,0},{2,3},{3,2},{4,5},{5,4},{6,7},{7,6},{8,9},{9,8},{10,11... | collective-permute-start | bytes 221192 | tf_op jit(solution)/shard_map/ppermute | solution.py:401
